TPU v7x, 32 devices: a whole 2x2x4 slice. The times are simulated.
32 devices in a mesh: dp: 2 (over x), row: 4 (over y, core), col: 4 (over z).
Axes of the slice: x: 2, y: 2, z: 4, core: 2. Of those that a mesh axis runs over, the one named last changes fastest.
Arguments:
- tokens: bfloat16 [6304, 512], P(('dp', 'row'), 'col'), may hold values from -9 to 9
- cotangent: bfloat16 [6304, 512], P(('dp', 'row'), 'col'), may hold values from -6 to 6
- expert_ids: int32 [6304, 2], P(('dp', 'row')), may hold values from 0 to 3, all different within a row
- priority: int32 [8, 788], P(('dp', 'row')), may hold values from 0 to 787, each once within a row
- qkv_weight: bfloat16 [512, 3, 512], P('col', None, 'row'), may hold values from -0.25 to 0.25
- out_weight: bfloat16 [512, 512], P('row', 'col'), may hold values from -2 to 2
- attn_gain: bfloat16 [512], P('col'), may hold values from 0.5 to 1.5
- attn_shift: bfloat16 [512], P('col'), may hold values from -0.5 to 0.5
- moe_gain: bfloat16 [512], P('col'), may hold values from 0.5 to 1.5
- moe_shift: bfloat16 [512], P('col'), may hold values from -0.5 to 0.5
- router: bfloat16 [512, 4], P('col'), may hold values from -0.1875 to 0.1875
- up_weight: bfloat16 [4, 512, 2048], P('dp', 'col', 'row'), may hold values from -0.25 to 0.25
- down_weight: bfloat16 [4, 2048, 512], P('dp', 'row', 'col'), may hold values from -0.1875 to 0.1875
Outputs:
- block_out: bfloat16 [6304, 512], P(('dp', 'row'), 'col')
- tokens_grad: bfloat16 [6304, 512], P(('dp', 'row'), 'col')
- qkv_grad: float32 [512, 3, 512], P('col', None, 'row')
- out_grad: float32 [512, 512], P('row', 'col')
- attn_gain_grad: float32 [512], P('col')
- attn_shift_grad: float32 [512], P('col')
- moe_gain_grad: float32 [512], P('col')
- moe_shift_grad: float32 [512], P('col')
- router_grad: float32 [512, 4], P('col')
- up_grad: float32 [4, 512, 2048], P('dp', 'col', 'row')
- down_grad: float32 [4, 2048, 512], P('dp', 'row', 'col')
- stream_rms: float32 [5], replicated
Inputs may be any that keep to these rules, and one draw needn't show every extreme that they name: `expert_ids`: each row names 2 different experts. `priority`: each row holds every token index of its block of 788 tokens once.
All inputs are finite; a program needn't handle non-finite values.
Results may differ from a plain program's by a relative error of at most 0.014.
Values may be sent and summed in bfloat16 or wider, within the bound.
No kernel may reach another device: no remote copies, remote signals or barrier semaphores. Data moves between devices by JAX's collectives and lax.ppermute only.
A program may use at most 128 MiB of HBM per device.

v0:
```python
import jax
import jax.numpy as jnp
from jax import lax
from jax.sharding import PartitionSpec as P

D = 512
HDIM = 64
SEQ = 197
E_DEV = 2
TOPK = 2


epsilon = 1e-06


def placement(choice_ids, priority_row, experts, capacity):
    token_count = priority_row.shape[0]
    ranked = jnp.take(choice_ids, priority_row, axis=0)
    pair_expert = jnp.concatenate([ranked[:, 0], ranked[:, 1]])
    onehot = (pair_expert[:, None] == jnp.arange(experts, dtype=jnp.int32)[None, :]).astype(
        jnp.int32
    )
    earlier = jnp.cumsum(onehot, axis=0) - onehot
    slot_rank = jnp.sum(earlier * onehot, axis=1)
    slot_index = jnp.where(
        slot_rank < capacity, slot_rank * experts + pair_expert, experts * capacity
    )
    per_token = (
        jnp.zeros((token_count, 2), jnp.int32)
        .at[priority_row]
        .set(jnp.stack([slot_index[:token_count], slot_index[token_count:]], axis=1))
    )
    pair_index = jnp.arange(2 * token_count, dtype=jnp.int32)
    holder = (
        jnp.full((experts * capacity,), 2 * token_count, jnp.int32)
        .at[per_token.reshape(-1)]
        .set(pair_index, mode="drop")
    )
    return (per_token, holder)


def gather_rows(values):
    return lax.all_gather(values, "row", axis=0, tiled=True)


def gather_cols(values):
    return lax.all_gather(values, "col", axis=0, tiled=True)


def reduce_cols(term_fn, local_rows):
    return lax.psum_scatter(
        term_fn(jnp.int32(0), local_rows * lax.axis_size("col")),
        "col",
        scatter_dimension=0,
        tiled=True,
    )


def reduce_rows(term_fn, local_rows):
    return lax.psum_scatter(
        term_fn(jnp.int32(0), local_rows * lax.axis_size("row")),
        "row",
        scatter_dimension=0,
        tiled=True,
    )


def width_totals(values):
    return lax.psum(values, "col")


def send_slots(values):
    return lax.all_to_all(values, "dp", split_axis=1, concat_axis=0, tiled=True)


def return_slots(values):
    return lax.all_to_all(values, "dp", split_axis=0, concat_axis=1, tiled=True)


def record(values, square_sums):
    square_sums.append(jnp.sum(values * values))


def norm_forward(values, norm_gain, norm_shift, total_width):
    sums_both = total_width(jnp.stack([jnp.sum(values, axis=1), jnp.sum(values * values, axis=1)]))
    center = sums_both[0] / D
    spread = sums_both[1] / D - center * center
    inverse = lax.rsqrt(spread + epsilon)
    normed = (values - center[:, None]) * inverse[:, None]
    return (normed, inverse, (normed * norm_gain + norm_shift).astype(jnp.bfloat16))


def norm_backward(grad_normed, normed, inverse, norm_gain, total_width):
    scaled = grad_normed * norm_gain
    sums_both = total_width(jnp.stack([jnp.sum(scaled, axis=1), jnp.sum(scaled * normed, axis=1)]))
    grad_values = inverse[:, None] * (
        scaled - sums_both[0][:, None] / D - normed * sums_both[1][:, None] / D
    )
    return (grad_values, jnp.sum(grad_normed * normed, axis=0), jnp.sum(grad_normed, axis=0))


def gate_from(logits, choice_ids):
    chosen = jnp.take_along_axis(logits, choice_ids, axis=1)
    raised = jnp.exp(chosen - jnp.max(chosen, axis=1, keepdims=True))
    return raised / jnp.sum(raised, axis=1, keepdims=True)


def logit_grads(gate_values, grad_gate, choice_ids, experts):
    grad_chosen = gate_values * (
        grad_gate - jnp.sum(gate_values * grad_gate, axis=1, keepdims=True)
    )
    expert_hits = (
        choice_ids[:, :, None] == jnp.arange(experts, dtype=jnp.int32)[None, None, :]
    ).astype(jnp.float32)
    return jnp.sum(expert_hits * grad_chosen[:, :, None], axis=1).astype(jnp.bfloat16)


def attend_forward(pieces, score_scale):
    queries, key_rows, values = pieces
    scores = (
        jnp.einsum("bqhd,bkhd->bhqk", queries, key_rows, preferred_element_type=jnp.float32)
        * score_scale
    )
    row_peak = jnp.max(scores, axis=-1, keepdims=True)
    raised = jnp.exp(scores - row_peak)
    row_total = jnp.sum(raised, axis=-1, keepdims=True)
    weights = (raised / row_total).astype(jnp.bfloat16)
    mixed_rows = jnp.einsum("bhqk,bkhd->bqhd", weights, values, preferred_element_type=jnp.float32)
    return (mixed_rows.astype(jnp.bfloat16), row_peak[..., 0] + jnp.log(row_total[..., 0]))


def attend_backward(pieces, score_scale):
    queries, key_rows, values, logsum, grad_mixed = pieces
    scores = (
        jnp.einsum("bqhd,bkhd->bhqk", queries, key_rows, preferred_element_type=jnp.float32)
        * score_scale
    )
    weights = jnp.exp(scores - logsum[..., None])
    grad_weights = jnp.einsum(
        "bqhd,bkhd->bhqk", grad_mixed, values, preferred_element_type=jnp.float32
    )
    grad_values = jnp.einsum(
        "bhqk,bqhd->bkhd",
        weights.astype(jnp.bfloat16),
        grad_mixed,
        preferred_element_type=jnp.float32,
    )
    grad_scores = (
        weights * (grad_weights - jnp.sum(weights * grad_weights, axis=-1, keepdims=True))
    ).astype(jnp.bfloat16)
    grad_queries = (
        jnp.einsum("bhqk,bkhd->bqhd", grad_scores, key_rows, preferred_element_type=jnp.float32)
        * score_scale
    )
    grad_keys = (
        jnp.einsum("bhqk,bqhd->bkhd", grad_scores, queries, preferred_element_type=jnp.float32)
        * score_scale
    )
    return jnp.stack([grad_queries, grad_keys, grad_values], axis=2)


def body(
    tokens,
    cotangent,
    expert_ids,
    priority,
    qkv_weight,
    out_weight,
    attn_gain,
    attn_shift,
    moe_gain,
    moe_shift,
    router,
    up_weight,
    down_weight,
):
    rows_sh, width_c = tokens.shape
    data_groups = lax.axis_size("dp")
    cols_axis = lax.axis_size("col")
    rows_axis = lax.axis_size("row")
    experts = data_groups * E_DEV
    capacity = cols_axis * max(
        1, (5 * TOPK * rows_sh + 4 * experts * cols_axis - 1) // (4 * experts * cols_axis)
    )
    score_scale = HDIM ** (-0.5)
    contract_rows = (((0,), (0,)), ((), ()))
    contract_cols = (((1,), (1,)), ((), ()))
    square_sums = []
    per_token, holder = placement(expert_ids, priority[0], experts, capacity)
    local_heads = qkv_weight.shape[2] // HDIM
    stream = tokens.astype(jnp.float32)
    record(stream, square_sums)
    normed_one, inverse_one, first_normed = norm_forward(
        stream, attn_gain, attn_shift, width_totals
    )
    first_gathered = gather_rows(first_normed)
    joint_weight = qkv_weight.reshape(width_c, -1)
    mixed_in = reduce_cols(
        lambda first_row, row_count: jnp.dot(
            first_gathered, joint_weight, preferred_element_type=jnp.float32
        ),
        rows_sh,
    ).astype(jnp.bfloat16)
    blocks = mixed_in.reshape(rows_sh // (2 * SEQ), 2, SEQ, 3, local_heads, HDIM)
    queries = blocks[:, :, :, 0]
    key_rows = blocks[:, :, :, 1]
    values = blocks[:, :, :, 2]
    attended, logsum = lax.map(
        lambda pieces: attend_forward(pieces, score_scale), (queries, key_rows, values)
    )
    attended = attended.reshape(rows_sh, -1)
    attended_all = gather_cols(attended)
    branch = reduce_rows(
        lambda first_row, row_count: jnp.dot(
            attended_all, out_weight, preferred_element_type=jnp.float32
        ),
        rows_sh,
    )
    record(branch, square_sums)
    middle = stream + branch
    record(middle, square_sums)
    normed_two, inverse_two, second_normed = norm_forward(middle, moe_gain, moe_shift, width_totals)
    logits = width_totals(jnp.dot(second_normed, router, preferred_element_type=jnp.float32))
    gate_values = gate_from(logits, expert_ids)
    padded = jnp.concatenate([second_normed, jnp.zeros((1, width_c), jnp.bfloat16)], axis=0)
    buffer = padded[holder // 2].reshape(capacity, data_groups, E_DEV, width_c)
    inputs = send_slots(buffer)
    slot_rows = inputs.shape[0]
    inputs_all = gather_rows(inputs)
    hidden_pre = reduce_cols(
        lambda first_row, row_count: jnp.einsum(
            "sged,edf->sgef", inputs_all, up_weight, preferred_element_type=jnp.float32
        ),
        slot_rows,
    )
    hidden_all = gather_cols(jax.nn.gelu(hidden_pre, approximate=False).astype(jnp.bfloat16))
    expert_made = reduce_rows(
        lambda first_row, row_count: jnp.einsum(
            "sgef,efd->sged", hidden_all, down_weight, preferred_element_type=jnp.float32
        ),
        slot_rows,
    ).astype(jnp.bfloat16)
    returned = return_slots(expert_made)
    flat_rows = jnp.concatenate(
        [returned.reshape(-1, width_c), jnp.zeros((1, width_c), jnp.bfloat16)], axis=0
    )
    picked = flat_rows[per_token].astype(jnp.float32)
    mixture = jnp.sum(gate_values[:, :, None] * picked, axis=1)
    record(mixture, square_sums)
    output = middle + mixture
    record(output, square_sums)
    grad_out = cotangent.astype(jnp.float32)
    grad_gate = width_totals(jnp.sum(grad_out[:, None, :] * picked, axis=2))
    grad_logits = logit_grads(gate_values, grad_gate, expert_ids, experts)
    router_part = lax.dot_general(
        grad_logits, router, contract_cols, preferred_element_type=jnp.float32
    )
    router_grad = lax.dot_general(
        second_normed, grad_logits, contract_rows, preferred_element_type=jnp.float32
    )
    pair_grads = (
        (gate_values[:, :, None] * grad_out[:, None, :]).astype(jnp.bfloat16).reshape(-1, width_c)
    )
    pair_grads = jnp.concatenate([pair_grads, jnp.zeros((1, width_c), jnp.bfloat16)], axis=0)
    grad_buffer = pair_grads[holder].reshape(capacity, data_groups, E_DEV, width_c)
    grad_inputs = send_slots(grad_buffer)
    grad_made_all = gather_rows(grad_inputs)
    down_grad = jnp.einsum(
        "sgef,sged->efd", hidden_all, grad_made_all, preferred_element_type=jnp.float32
    )
    grad_hidden = reduce_cols(
        lambda first_row, row_count: jnp.einsum(
            "sged,efd->sgef", grad_made_all, down_weight, preferred_element_type=jnp.float32
        ),
        slot_rows,
    )
    unused_value, gelu_back = jax.vjp(
        lambda pre_values: jax.nn.gelu(pre_values, approximate=False), hidden_pre
    )
    grad_pre = gelu_back(grad_hidden)[0].astype(jnp.bfloat16)
    grad_pre_all = gather_cols(grad_pre)
    up_grad = jnp.einsum(
        "sged,sgef->edf", inputs_all, grad_pre_all, preferred_element_type=jnp.float32
    )
    grad_slots_in = reduce_rows(
        lambda first_row, row_count: jnp.einsum(
            "sgef,edf->sged", grad_pre_all, up_weight, preferred_element_type=jnp.float32
        ),
        slot_rows,
    ).astype(jnp.bfloat16)
    grad_returned = return_slots(grad_slots_in)
    grad_flat = jnp.concatenate(
        [grad_returned.reshape(-1, width_c), jnp.zeros((1, width_c), jnp.bfloat16)], axis=0
    )
    grad_second = jnp.sum(grad_flat[per_token].astype(jnp.float32), axis=1) + router_part
    grad_middle_norm, moe_gain_grad, moe_shift_grad = norm_backward(
        grad_second, normed_two, inverse_two, moe_gain, width_totals
    )
    grad_middle = grad_out + grad_middle_norm
    grad_branch_all = gather_rows(grad_middle.astype(jnp.bfloat16))
    out_grad = lax.dot_general(
        attended_all, grad_branch_all, contract_rows, preferred_element_type=jnp.float32
    )
    grad_attended = reduce_cols(
        lambda first_row, row_count: lax.dot_general(
            grad_branch_all, out_weight, contract_cols, preferred_element_type=jnp.float32
        ),
        rows_sh,
    ).astype(jnp.bfloat16)
    grad_blocks = grad_attended.reshape(rows_sh // (2 * SEQ), 2, SEQ, local_heads, HDIM)
    grad_mixed = lax.map(
        lambda pieces: attend_backward(pieces, score_scale),
        (queries, key_rows, values, logsum, grad_blocks),
    )
    grad_mixed = grad_mixed.reshape(rows_sh, -1).astype(jnp.bfloat16)
    grad_mixed_all = gather_cols(grad_mixed)
    qkv_grad = lax.dot_general(
        first_gathered, grad_mixed_all, contract_rows, preferred_element_type=jnp.float32
    ).reshape(width_c, 3, -1)
    grad_first = reduce_rows(
        lambda first_row, row_count: lax.dot_general(
            grad_mixed_all, joint_weight, contract_cols, preferred_element_type=jnp.float32
        ),
        rows_sh,
    )
    grad_stream_norm, attn_gain_grad, attn_shift_grad = norm_backward(
        grad_first, normed_one, inverse_one, attn_gain, width_totals
    )
    tokens_grad = (grad_middle + grad_stream_norm).astype(jnp.bfloat16)
    block_out = output.astype(jnp.bfloat16)
    qkv_grad, out_grad = lax.psum((qkv_grad, out_grad), "dp")
    attn_gain_grad, attn_shift_grad, moe_gain_grad, moe_shift_grad, router_grad = lax.psum(
        (attn_gain_grad, attn_shift_grad, moe_gain_grad, moe_shift_grad, router_grad), ("dp", "row")
    )
    totals = jnp.stack(
        lax.psum(
            (square_sums[0], square_sums[1], square_sums[2], square_sums[3], square_sums[4]),
            ("dp", "row", "col"),
        )
    )
    entry_count = rows_sh * data_groups * rows_axis * width_c * cols_axis
    stream_rms = jnp.sqrt(totals / entry_count)
    return (
        block_out,
        tokens_grad,
        qkv_grad,
        out_grad,
        attn_gain_grad,
        attn_shift_grad,
        moe_gain_grad,
        moe_shift_grad,
        router_grad,
        up_grad,
        down_grad,
        stream_rms,
    )


def solution(mesh):
    in_specs = (
        P(("dp", "row"), "col"),
        P(("dp", "row"), "col"),
        P(("dp", "row"), None),
        P(("dp", "row"), None),
        P("col", None, "row"),
        P("row", "col"),
        P("col"),
        P("col"),
        P("col"),
        P("col"),
        P("col", None),
        P("dp", "col", "row"),
        P("dp", "row", "col"),
    )
    out_specs = (
        P(("dp", "row"), "col"),
        P(("dp", "row"), "col"),
        P("col", None, "row"),
        P("row", "col"),
        P("col"),
        P("col"),
        P("col"),
        P("col"),
        P("col", None),
        P("dp", "col", "row"),
        P("dp", "row", "col"),
        P(),
    )
    return jax.shard_map(body, mesh=mesh, in_specs=in_specs, out_specs=out_specs, check_vma=False)
```

profile of v0, /device:TPU:0, one launch (start us, length us, event | category | flops | bytes accessed | tf_op | source)
XLA Modules:
  0.0 1518.2 jit_solution(11945377452013760286)
XLA Ops:
  8.5 13.7 psum.126
  24.9 8.8 all-gather
  35.6 3.2 fusion.110
  38.7 87.1 %fusion = f32[800,384]{1,0:T(8,128)S(1)} fusion(f32[3152,384]{1,0:T(8,128)} %fusion.110), kind=kCustom, calls=%all-reduce-scatter | all-reduce-scatter fusion | flops 1228801 | bytes 6070784
  132.8 4.2 scatter_custom_fusion
  137.4 8.8 scatter_custom_fusion.1
  154.9 17.8 %all-gather.1 = bf16[4,788,128]{2,1,0:T(8,128)(2,1)S(1)} all-gather(bf16[1,788,128]{2,1,0:T(8,128)(2,1)S(1)} %reshape.380), channel_id=1, replica_groups=mesh['dp'=2,'row'=4,'col'=4] {'col'}, dimensions={0}, use_global_device_ids=true | all-gather | bytes 1008640 | tf_op jit(solution)/shard_map/all_gather | solution.py:47
  173.4 19.2 %fusion.1 = f32[800,128]{1,0:T(8,128)} fusion(f32[3152,128]{1,0:T(8,128)S(1)} %fusion.111), kind=kCustom, calls=%all-reduce-scatter.1 | all-reduce-scatter fusion | flops 409601 | bytes 2023936
  198.1 11.0 psum.127
  209.5 6.3 gather_fusion.1
  216.0 9.9 all_to_all.66
  227.4 15.6 %psum.128 = f32[788,4]{0,1:T(4,128)S(1)} all-reduce(f32[788,4]{0,1:T(4,128)S(1)} %fusion.112), channel_id=1, replica_groups=mesh['dp'=2,'row'=4,'col'=4] {'col'}, use_global_device_ids=true, to_apply=%region_12.13 | all-reduce | flops 3152 | bytes 25216 | tf_op jit(solution)/shard_map/psum | solution.py:69
  243.0 19.7 %gather_fusion.5 = f32[1576]{0:T(1024)S(1)} fusion(f32[788,4]{0,1:T(4,128)S(1)} %psum.128, s32[1576]{0:T(1024)S(1)} %reshape.335), kind=kCustom, calls=%fused_computation.5 | custom fusion | bytes 25216 | tf_op jit(solution)/shard_map/jit(take_along_axis)/gather | solution.py:103
  264.3 6.3 gather_fusion.3
  270.7 8.9 all_to_all.67
  280.5 9.8 convolution_bitcast_fusion.2
  290.3 10.7 all-gather.14.cloned.1.call-done
  301.0 10.0 convolution_bitcast_fusion.1
  311.2 264.3 %reduce-scatter.13.cloned.1.call-done = f32[992,1,2,512]{3,0,2,1:T(8,128)} async-done(((f32[3968,1,2,512]{3,0,2,1:T(8,128)}), f32[992,1,2,512]{3,0,2,1:T(8,128)}) %reduce-scatter.13.cloned.1.call-update) | async-done | bytes 4063248 | tf_op jit(solution)/shard_map/reduce_scatter | solution.py:51
  575.5 274.9 %reduce-scatter.17.cloned.1.call-done = f32[992,1,2,512]{3,0,2,1:T(8,128)} async-done(((f32[3968,1,2,512]{3,0,2,1:T(8,128)}), f32[992,1,2,512]{3,0,2,1:T(8,128)}) %reduce-scatter.17.cloned.1.call-update) | async-done | bytes 4063248 | tf_op jit(solution)/shard_map/reduce_scatter | solution.py:51
  850.4 12.0 add_convert_fusion
  865.5 145.4 %all-gather.12.cloned.1.call-done = bf16[3968,1,2,512]{3,0,2,1:T(8,128)(2,1)} async-done(((bf16[992,1,2,512]{3,0,2,1:T(8,128)(2,1)}), bf16[3968,1,2,512]{3,0,2,1:T(8,128)(2,1)}) %all-gather.12.cloned.1.call-update) | async-done | bytes 8126480 | tf_op jit(solution)/shard_map/all_gather | solution.py:47
  1010.9 7.5 fusion.49
  1018.5 137.4 %all-gather.16.cloned.1.call-done = bf16[3968,1,2,512]{3,0,2,1:T(8,128)(2,1)} async-done(((bf16[992,1,2,512]{3,0,2,1:T(8,128)(2,1)}), bf16[3968,1,2,512]{3,0,2,1:T(8,128)(2,1)}) %all-gather.16.cloned.1.call-update) | async-done | bytes 8126480 | tf_op jit(solution)/shard_map/all_gather | solution.py:47
  1155.9 7.5 fusion.52
  1164.7 35.7 %reduce-scatter.15.cloned.1.call-done = f32[992,1,2,128]{3,0,2,1:T(8,128)} async-done(((f32[3968,1,2,128]{3,0,2,1:T(8,128)}), f32[992,1,2,128]{3,0,2,1:T(8,128)}) %reduce-scatter.15.cloned.1.call-update) | async-done | bytes 1015824 | tf_op jit(solution)/shard_map/reduce_scatter | solution.py:60
  1202.8 3.5 all-to-all-start.1
  1206.8 40.0 %reduce-scatter.19.cloned.1.call-done = f32[992,1,2,128]{3,0,2,1:T(8,128)} async-done(((f32[3968,1,2,128]{3,0,2,1:T(8,128)}), f32[992,1,2,128]{3,0,2,1:T(8,128)}) %reduce-scatter.19.cloned.1.call-update) | async-done | bytes 1015824 | tf_op jit(solution)/shard_map/reduce_scatter | solution.py:60
  1249.2 3.5 all-to-all-start.3
  1253.2 3.8 gather_fusion.2
  1257.0 4.8 fusion.66
  1262.0 12.1 psum.129
  1274.6 3.8 gather_fusion.4
  1281.6 8.5 psum.130
  1291.3 7.8 all-gather.2
  1301.0 35.2 %fusion.2 = f32[800,128]{1,0:T(8,128)S(1)} fusion(f32[3152,128]{1,0:T(8,128)} %fusion.113), kind=kCustom, calls=%all-reduce-scatter.2 | all-reduce-scatter fusion | flops 409601 | bytes 2023936
  1341.3 4.9 while.23
  1346.2 3.9 copy.280
  1350.1 3.5 reshape.382
  1353.9 5.6 fusion.41
  1359.6 8.0 fusion.45
  1368.8 36.6 %all-gather.18.cloned.1.call-done = bf16[4,788,384]{2,1,0:T(8,128)(2,1)} async-done(((bf16[1,788,384]{2,1,0:T(8,128)(2,1)}), bf16[4,788,384]{2,1,0:T(8,128)(2,1)}) %all-gather.18.cloned.1.call-update) | async-done | bytes 2420752 | tf_op jit(solution)/shard_map/all_gather | solution.py:47
  1407.4 3.2 fusion.114
  1410.5 20.2 %fusion.3 = f32[800,128]{1,0:T(8,128)} fusion(f32[3152,128]{1,0:T(8,128)} %fusion.114), kind=kCustom, calls=%all-reduce-scatter.3 | all-reduce-scatter fusion | flops 409601 | bytes 2023936
  1438.0 40.4 %all-reduce.13 = (f32[1]{0:T(128)}, f32[1]{0:T(128)}, f32[1]{0:T(128)}, f32[1]{0:T(128)}, f32[1]{0:T(128)}) all-reduce(f32[1]{0:T(128)} %bitcast.62, f32[1]{0:T(128)} %bitcast.63, f32[1]{0:T(128)} %bitcast.64, f32[1]{0:T(128)} %bitcast.65, f32[1]{0:T(128)} %bitcast.66), channel_id=1, replica_groups=mesh['dp'=2,'row'=4,'col'=4] {'dp','row','col'}, use_global_device_ids=true, to_apply=%region_53.54 | all-reduce | flops 5 | bytes 40 | tf_op jit(solution)/shard_map/psum | solution.py:336
  1478.4 3.3 stack.95
  1482.3 10.8 psum.131
  1493.1 12.4 all-reduce.14
  (289 shorter events, 75.8 us)
Async XLA Ops:
  7.2 293.8 %copy-start = (bf16[2,512,128]{2,1,0:T(8,128)(2,1)S(1)}, bf16[2,512,128]{2,1,0:T(8,128)(2,1)}, u32[]{:S(2)}) copy-start(bf16[2,512,128]{2,1,0:T(8,128)(2,1)} %param.29) | copy-start | bytes 786436
  7.2 273.3 %all-gather.10.cloned.1.call-start = ((), (), s32[]{:S(2)}) async-start(), calls=%async_computation.8 | async-start | bytes 2539520 | tf_op jit(solution)/shard_map/all_gather | solution.py:43
  38.7 89.1 %copy-start.37 = (s32[1,788]{1,0:T(1,128)S(1)}, s32[1,788]{1,0:T(1,128)}, u32[]{:S(2)}) copy-start(s32[1,788]{1,0:T(1,128)} %param.20) | copy-start | bytes 9460
  38.7 89.2 %copy-start.26 = (s32[788,2]{0,1:T(2,128)S(1)}, s32[788,2]{0,1:T(2,128)}, u32[]{:S(2)}) copy-start(s32[788,2]{0,1:T(2,128)} %param.19) | copy-start | bytes 18916
  125.8 20.4 %copy-start.45 = (u32[32]{0:T(128)S(1)}, u32[32]{0:T(128)}, u32[]{:S(2)}) copy-start(u32[32]{0:T(128)} %constant.224) | copy-start | bytes 388
  125.9 21.6 %collective-permute-start = (bf16[36,384]{1,0:T(8,128)(2,1)S(1)}, bf16[36,384]{1,0:T(8,128)(2,1)S(1)}, u32[]{:S(2)}, u32[]{:S(2)}) collective-permute-start(bf16[36,384]{1,0:T(8,128)(2,1)S(1)} %slice.101), channel_id=1, source_target_pairs={{0,1},{1,2},{2,3},{4,5},{5,6},{6,7},{8,9},{9,10},{10,11},{12,13},{... | collective-permute-start | bytes 82952
  152.4 20.4 %copy-start.24 = (bf16[128,128]{1,0:T(8,128)(2,1)S(1)}, bf16[128,128]{1,0:T(8,128)(2,1)}, u32[]{:S(2)}) copy-start(bf16[128,128]{1,0:T(8,128)(2,1)} %param.22) | copy-start | bytes 98308
  154.0 38.5 %copy-start.2 = (bf16[2,2,197,2,64]{2,4,3,1,0:T(8,128)(2,1)}, bf16[2,2,197,2,64]{2,4,3,1,0:T(8,128)(2,1)S(1)}, u32[]{:S(2)}) copy-start(bf16[2,2,197,2,64]{2,4,3,1,0:T(8,128)(2,1)S(1)} %get-tuple-element.499) | copy-start | bytes 605188
  154.0 38.5 %copy-start.4 = (bf16[2,2,197,2,64]{2,4,3,1,0:T(8,128)(2,1)}, bf16[2,2,197,2,64]{2,4,3,1,0:T(8,128)(2,1)S(1)}, u32[]{:S(2)}) copy-start(bf16[2,2,197,2,64]{2,4,3,1,0:T(8,128)(2,1)S(1)} %get-tuple-element.500) | copy-start | bytes 605188
  154.1 40.6 %copy-start.44 = (u32[32]{0:T(128)S(1)}, u32[32]{0:T(128)}, u32[]{:S(2)}) copy-start(u32[32]{0:T(128)} %constant.228) | copy-start | bytes 388
  154.6 41.3 %copy-start.46 = (bf16[128]{0:T(256)(128)(2,1)S(1)}, bf16[128]{0:T(256)(128)(2,1)}, u32[]{:S(2)}) copy-start(bf16[128]{0:T(256)(128)(2,1)} %param.25) | copy-start | bytes 772
  154.6 41.3 %copy-start.47 = (bf16[128]{0:T(256)(128)(2,1)S(1)}, bf16[128]{0:T(256)(128)(2,1)}, u32[]{:S(2)}) copy-start(bf16[128]{0:T(256)(128)(2,1)} %param.26) | copy-start | bytes 772
  154.8 42.5 %copy-start.14 = (bf16[788,128]{1,0:T(8,128)(2,1)S(1)}, bf16[788,128]{1,0:T(8,128)(2,1)}, u32[]{:S(2)}) copy-start(bf16[788,128]{1,0:T(8,128)(2,1)} %param.17) | copy-start | bytes 605188
  172.8 43.1 %copy-start.10 = (bf16[3152,128]{1,0:T(8,128)(2,1)}, bf16[3152,128]{1,0:T(8,128)(2,1)S(1)}, u32[]{:S(2)}) copy-start(bf16[3152,128]{1,0:T(8,128)(2,1)S(1)} %reshape.373) | copy-start | bytes 2420740
  193.3 2.6 collective-permute-start.1
  195.9 20.0 %copy-start.40 = (f32[128]{0:T(128)}, f32[128]{0:T(128)S(1)}, u32[]{:S(2)}) copy-start(f32[128]{0:T(128)S(1)} %convert_element_type.97) | copy-start | bytes 1540
  209.2 17.5 %copy-start.29 = (f32[788]{0:T(1024)}, f32[788]{0:T(1024)S(1)}, u32[]{:S(2)}) copy-start(f32[788]{0:T(1024)S(1)} %get-tuple-element.269) | copy-start | bytes 9460
  209.2 17.5 %copy-start.33 = (f32[788]{0:T(1024)}, f32[788]{0:T(1024)S(1)}, u32[]{:S(2)}) copy-start(f32[788]{0:T(1024)S(1)} %add_rsqrt_fusion) | copy-start | bytes 9460
  209.5 17.7 %copy-start.17 = (bf16[788,128]{1,0:T(8,128)(2,1)}, bf16[788,128]{1,0:T(8,128)(2,1)S(1)}, u32[]{:S(2)}) copy-start(bf16[788,128]{1,0:T(8,128)(2,1)S(1)} %add_convert_fusion.1) | copy-start | bytes 605188
  209.5 17.7 %copy-start.42 = (bf16[128,4]{0,1:T(4,128)(2,1)S(1)}, bf16[128,4]{0,1:T(4,128)(2,1)}, u32[]{:S(2)}) copy-start(bf16[128,4]{0,1:T(4,128)(2,1)} %param.27) | copy-start | bytes 3076
  226.7 74.3 %all-gather.14.cloned.1.call-start = ((), (), s32[]{:S(2)}) async-start(), calls=%async_computation.12 | async-start | bytes 2539520 | tf_op jit(solution)/shard_map/all_gather | solution.py:43
  243.0 20.7 %copy-start.21 = (bf16[788,128]{1,0:T(8,128)(2,1)S(1)}, bf16[788,128]{1,0:T(8,128)(2,1)}, u32[]{:S(2)}) copy-start(bf16[788,128]{1,0:T(8,128)(2,1)} %param.18) | copy-start | bytes 605188
  280.4 295.1 %reduce-scatter.13.cloned.1.call-start = ((), (), s32[]{:S(2)}) async-start(), calls=%async_computation.9 | async-start | bytes 20316160 | tf_op jit(solution)/shard_map/reduce_scatter | solution.py:51
  290.3 560.1 %reduce-scatter.17.cloned.1.call-start = ((), (), s32[]{:S(2)}) async-start(), calls=%async_computation.13 | async-start | bytes 20316160 | tf_op jit(solution)/shard_map/reduce_scatter | solution.py:51
  311.0 699.9 %all-gather.12.cloned.1.call-start = ((), (), s32[]{:S(2)}) async-start(), calls=%async_computation.10 | async-start | bytes 10158080 | tf_op jit(solution)/shard_map/all_gather | solution.py:47
  864.9 291.0 %all-gather.16.cloned.1.call-start = ((), (), s32[]{:S(2)}) async-start(), calls=%async_computation.14 | async-start | bytes 10158080 | tf_op jit(solution)/shard_map/all_gather | solution.py:47
  865.5 334.9 %reduce-scatter.15.cloned.1.call-start = ((), (), s32[]{:S(2)}) async-start(), calls=%async_computation.11 | async-start | bytes 5079040 | tf_op jit(solution)/shard_map/reduce_scatter | solution.py:60
  1018.4 228.3 %reduce-scatter.19.cloned.1.call-start = ((), (), s32[]{:S(2)}) async-start(), calls=%async_computation.15 | async-start | bytes 5079040 | tf_op jit(solution)/shard_map/reduce_scatter | solution.py:60
  1202.8 46.4 %all-to-all-start.1 = ((bf16[992,1,2,128]{3,2,1,0:T(2,128)(2,1)}), bf16[992,1,2,128]{3,2,1,0:T(2,128)(2,1)S(1)}, u32[]{:S(2)}, u32[]{:S(2)}) async-start(bf16[992,1,2,128]{3,2,1,0:T(2,128)(2,1)} %copy.247), calls=%async_computation.3 | async-start | bytes 1015808 | tf_op jit(solution)/shard_map/all_to_all | solution.py:77
  1249.2 25.0 %all-to-all-start.3 = ((bf16[992,1,2,128]{3,2,1,0:T(2,128)(2,1)}), bf16[992,1,2,128]{3,2,1,0:T(2,128)(2,1)S(1)}, u32[]{:S(2)}, u32[]{:S(2)}) async-start(bf16[992,1,2,128]{3,2,1,0:T(2,128)(2,1)} %copy.256), calls=%async_computation.7 | async-start | bytes 1015808 | tf_op jit(solution)/shard_map/all_to_all | solution.py:77
  1252.7 152.7 %all-gather.18.cloned.1.call-start = ((), (), s32[]{:S(2)}) async-start(), calls=%async_computation.16 | async-start | bytes 3041280 | tf_op jit(solution)/shard_map/all_gather | solution.py:47
  1261.8 17.9 %copy-start.13 = (f32[788,128]{1,0:T(8,128)S(1)}, f32[788,128]{1,0:T(8,128)}, u32[]{:S(2)}) copy-start(f32[788,128]{1,0:T(8,128)} %copy-done.12) | copy-start | bytes 1210372
  1261.8 17.9 %copy-start.30 = (f32[788]{0:T(1024)S(1)}, f32[788]{0:T(1024)}, u32[]{:S(2)}) copy-start(f32[788]{0:T(1024)} %copy-done.29) | copy-start | bytes 9460
  1261.8 17.9 %copy-start.34 = (f32[788]{0:T(1024)S(1)}, f32[788]{0:T(1024)}, u32[]{:S(2)}) copy-start(f32[788]{0:T(1024)} %copy-done.33) | copy-start | bytes 9460
  1261.8 17.9 %copy-start.41 = (f32[128]{0:T(128)S(1)}, f32[128]{0:T(128)}, u32[]{:S(2)}) copy-start(f32[128]{0:T(128)} %copy-done.40) | copy-start | bytes 1540
  1261.8 17.9 %copy-start.43 = (bf16[128,4]{0,1:T(4,128)(2,1)S(1)}, bf16[128,4]{0,1:T(4,128)(2,1)}, u32[]{:S(2)}) copy-start(bf16[128,4]{0,1:T(4,128)(2,1)} %param.27) | copy-start | bytes 3076
  1278.5 20.8 %copy-start.25 = (bf16[128,128]{1,0:T(8,128)(2,1)S(1)}, bf16[128,128]{1,0:T(8,128)(2,1)}, u32[]{:S(2)}) copy-start(bf16[128,128]{1,0:T(8,128)(2,1)} %param.22) | copy-start | bytes 98308
  1299.1 42.1 %copy-start.3 = (bf16[2,2,197,2,64]{2,4,3,1,0:T(8,128)(2,1)S(1)}, bf16[2,2,197,2,64]{2,4,3,1,0:T(8,128)(2,1)}, u32[]{:S(2)}) copy-start(bf16[2,2,197,2,64]{2,4,3,1,0:T(8,128)(2,1)} %copy-done.2) | copy-start | bytes 605188
  1299.1 42.1 %copy-start.5 = (bf16[2,2,197,2,64]{2,4,3,1,0:T(8,128)(2,1)S(1)}, bf16[2,2,197,2,64]{2,4,3,1,0:T(8,128)(2,1)}, u32[]{:S(2)}) copy-start(bf16[2,2,197,2,64]{2,4,3,1,0:T(8,128)(2,1)} %copy-done.4) | copy-start | bytes 605188
  1299.1 42.1 %copy-start.20 = (bf16[2,2,197,2,64]{2,4,3,1,0:T(8,128)(2,1)S(1)}, bf16[2,2,197,2,64]{2,4,3,1,0:T(8,128)(2,1)}, u32[]{:S(2)}) copy-start(bf16[2,2,197,2,64]{2,4,3,1,0:T(8,128)(2,1)} %copy-done.19) | copy-start | bytes 605188
  1299.1 42.1 %copy-start.36 = (f32[2,2,2,197]{3,2,1,0:T(2,128)S(1)}, f32[2,2,2,197]{3,2,1,0:T(2,128)}, u32[]{:S(2)}) copy-start(f32[2,2,2,197]{3,2,1,0:T(2,128)} %copy-done.35) | copy-start | bytes 18916
  1336.3 3.4 collective-permute-start.2
  1353.6 154.1 %all-reduce.18.cloned.1.call-start = ((), (), s32[]{:S(2)}) async-start(), calls=%async_computation.17 | async-start | bytes 524288 | tf_op jit(solution)/shard_map/psum | solution.py:331
  1407.4 25.4 %copy-start.8 = (bf16[3152,128]{1,0:T(8,128)(2,1)S(1)}, bf16[3152,128]{1,0:T(8,128)(2,1)}, u32[]{:S(2)}) copy-start(bf16[3152,128]{1,0:T(8,128)(2,1)} %copy-done.7) | copy-start | bytes 2420740
  1410.5 25.4 %copy-start.28 = (f32[788]{0:T(1024)S(1)}, f32[788]{0:T(1024)}, u32[]{:S(2)}) copy-start(f32[788]{0:T(1024)} %copy-done.27) | copy-start | bytes 9460
  1410.5 25.4 %copy-start.32 = (f32[788]{0:T(1024)S(1)}, f32[788]{0:T(1024)}, u32[]{:S(2)}) copy-start(f32[788]{0:T(1024)} %copy-done.31) | copy-start | bytes 9460
  1410.5 25.4 %copy-start.39 = (f32[128]{0:T(128)S(1)}, f32[128]{0:T(128)}, u32[]{:S(2)}) copy-start(f32[128]{0:T(128)} %copy-done.38) | copy-start | bytes 1540
  1431.4 3.1 collective-permute-start.3
  (16 other events, 97.9 us)
Sparse Core Ops, SparseCore 0:
  226.9 20.0 all-gather.9
  280.5 20.4 all-gather.13
  303.4 272.0 reduce-scatter.12
  577.7 272.6 reduce-scatter.16
  865.0 145.8 all-gather.11
  1012.3 143.5 all-gather.15
  1158.4 41.9 reduce-scatter.14
  1202.9 43.7 reduce-scatter.18
  1353.7 51.6 all-gather.17
  1434.6 22.5 all-reduce.17
where the time goes:
time: 1530 us; the launch traced here: 1520 us
  waiting for transfers between devices  947 us (62%)
  blocking collectives  339 us (22%)
  local copies, waits for them, and re-layouts  95.3 us (6%)
  matrix products  66.2 us (4%)
  other arithmetic  38.6 us (3%)
  between operations  17.3 us (1%)
    reduce_scatter x2, waiting for transfers between devices, reduce_cols(): lax.psum_scatter(term_fn(jnp.int32(0), local_rows * lax.axis_size('col'))...  539 us
    all_gather x3, waiting for transfers between devices, gather_cols(): return lax.all_gather(values, 'col', axis=0, tiled=True)  319 us
    unnamed x4, blocking collectives  162 us
    reduce_scatter x2, waiting for transfers between devices, reduce_rows(): lax.psum_scatter(term_fn(jnp.int32(0), local_rows * lax.axis_size('row'))...  75.7 us
    psum x6, blocking collectives, width_totals(): return lax.psum(values, 'col')  71.7 us
    psum x1, blocking collectives, body(): lax.psum((square_sums[0], square_sums[1], square_sums[2], square_sums[3],...  40.4 us
  transfers between devices with their start and end apart: 16, of which 9 were waited for; matrix products, arithmetic and copies ran while one was open for 8% of the time, Pallas kernels for 0%

commit v1 on v0

v1 whole, which is shorter than its diff:
```python
import jax
import jax.numpy as jnp
from jax import lax
from jax.experimental import pallas as pl
from jax.experimental.pallas import tpu as pltpu
from jax.sharding import PartitionSpec as P


D = 512
HDIM = 64
SEQ = 197
E_DEV = 2
TOPK = 2
epsilon = 1e-06
BF = jnp.bfloat16
F32 = jnp.float32
PLANE = ("dp", "row")


def round_up(value, step):
    return -(-value // step) * step


def swap(value, axis, offset):
    size = lax.axis_size(axis)
    return lax.ppermute(value, axis, [(i, i ^ offset) for i in range(size)])


def exchange(pieces, axis):
    return [pieces[0]] + [swap(pieces[s], axis, s) for s in range(1, len(pieces))]


def share(value, axis):
    return exchange([value] * lax.axis_size(axis), axis)


def nn(a, b):
    return jnp.dot(a, b, preferred_element_type=F32)


def nt(a, b):
    return lax.dot_general(a, b, (((1,), (1,)), ((), ())), preferred_element_type=F32)


def tn(a, b):
    return lax.dot_general(a, b, (((0,), (0,)), ((), ())), preferred_element_type=F32)


def plane_size():
    return lax.axis_size("dp") * lax.axis_size("row")


def plane_gather(block):
    count = plane_size()
    if count > 8:
        return [lax.all_gather(block, PLANE, axis=0)]
    far = [block] + [swap(block, PLANE, s) for s in range(2, count, 2)]
    far = jnp.stack(far)
    near = swap(far, PLANE, 1)
    return [far, near]


def plane_reduce(parts, pack):
    if len(parts) == 1:
        total = jnp.sum(lax.all_to_all(parts[0], PLANE, 0, 0, tiled=True).astype(F32), axis=0)
        return total[0], [total[1]]
    got = swap(parts[1], PLANE, 1)
    pieces = []
    for k in (0, 1):
        near = parts[0][:, k] + got[:, k].astype(F32)
        packed = pack(near[1:]) if k == 0 else near[1:].astype(BF)
        pieces.append([near[0]] + [swap(packed[s - 1], PLANE, 2 * s) for s in range(1, near.shape[0])])
    return add_up(pieces[0]), pieces[1]


def add_up(pieces):
    total = pieces[0]
    for piece in pieces[1:]:
        total = total + piece.astype(F32)
    return total


PER_STEP = 2


def expert_kernel(*refs, n_groups, n_col, step_counts, tail):
    x_refs, go_refs = refs[:n_groups], refs[n_groups : 2 * n_groups]
    refs = refs[2 * n_groups :]
    w_refs, (sel_ref,) = refs[:n_col], refs[n_col : n_col + 1]
    refs = refs[n_col + 1 :]
    out_refs, own_ref = refs[:n_groups], refs[n_groups]
    send_refs = refs[n_groups + 1 : n_groups + n_col]
    w_all, grads = refs[n_groups + n_col :]
    step = pl.program_id(0)
    width = w_refs[0].shape[1]
    rows = x_refs[0].shape[1]
    lanes = min(round_up(rows, 128), x_refs[0].shape[2])

    @pl.when(step == 0)
    def _():
        for s in range(n_col):
            w_all[:, pl.ds(s * width, width), :] = w_refs[s][...]
        grads[...] = jnp.zeros_like(grads)

    if n_groups == 2:
        first = step < step_counts[0]
        x = jnp.where(first, x_refs[0][...], x_refs[1][...])
        go = jnp.where(first, go_refs[0][...], go_refs[1][...])
    else:
        x, go = x_refs[0][...], go_refs[0][...]
    start = rows - tail
    x_tail = x[:, start:, :lanes]
    gate = jnp.concatenate(
        [tn(x_tail[b], sel_ref[0] + sel_ref[1])[:rows] for b in range(PER_STEP)], axis=0)
    x = x.reshape(PER_STEP * rows, -1)
    go = go.reshape(PER_STEP * rows, -1)
    up, down = w_all[0], w_all[1]
    pre = nn(x, up)
    back = nn(go, down)
    cdf = 0.5 * (1.0 + lax.erf(pre * (0.5**0.5)))
    slope = cdf + pre * (jnp.exp(-0.5 * pre * pre) * ((2.0 * jnp.pi) ** -0.5))
    hidden = pre * cdf
    product = hidden.astype(BF).astype(F32) * back
    gated = (gate * hidden).astype(BF)
    grad_pre = (gate * back * slope).astype(BF)
    grads[0] += tn(x, grad_pre)
    grads[1] += tn(go, gated)
    mix = nt(gated, down).reshape(PER_STEP, rows, -1)
    grad_x = nt(grad_pre, up).reshape(PER_STEP, rows, -1)
    p_high = product.astype(BF)
    p_low = (product - p_high.astype(F32)).astype(BF)

    def gate_rows(which, b):
        part = pl.ds(b * rows, rows)
        high, low = p_high[b * rows : (b + 1) * rows], p_low[b * rows : (b + 1) * rows]
        return nt(sel_ref[which], high) + nt(sel_ref[which], low)

    def spread(value):
        missing = x_refs[0].shape[2] - rows
        return jnp.concatenate([value, jnp.zeros((tail, missing), F32)], axis=1)

    def store(k, packed):
        out_refs[k][:, 1] = mix.astype(out_refs[k].dtype)
        out_refs[k][:, 0, :start] = grad_x[:, :start].astype(out_refs[k].dtype)
        for b in range(PER_STEP):
            high = spread(gate_rows(0, b))
            if packed:
                low = spread(gate_rows(1, b))
                low = low - low.astype(BF).astype(F32)
                value = (grad_x[b, start:] + high).astype(BF) + low.astype(BF)
            else:
                value = grad_x[b, start:] + high
            out_refs[k][b, 0, start:] = value

    if n_groups == 2:
        pl.when(first)(lambda: store(0, False))
        pl.when(jnp.logical_not(first))(lambda: store(1, True))
    else:
        store(0, True)

    @pl.when(step == sum(step_counts) - 1)
    def _():
        own_ref[...] = grads[:, :width]
        for s in range(1, n_col):
            send_refs[s - 1][...] = grads[:, s * width : (s + 1) * width].astype(BF)


def run_experts(x_groups, go_groups, weights, select, interpret=False):
    n_groups, n_col = len(x_groups), len(weights)
    _, rows, model = x_groups[0].shape
    tail = select.shape[1]
    counts = [g.shape[0] // PER_STEP for g in x_groups]
    firsts = [sum(counts[:k]) for k in range(n_groups)]
    _, width, wide = weights[0].shape

    def blocks(k, *extra):
        low, high = firsts[k], counts[k] - 1
        rest = (0,) * (len(extra) + 2)
        return pl.BlockSpec((PER_STEP, *extra, rows, model), lambda i: (jnp.clip(i - low, 0, high), *rest))

    def fixed(shape):
        return pl.BlockSpec(shape, lambda i: (0,) * len(shape))

    def kind(k):
        return BF if k == n_groups - 1 else F32

    total = sum(g.shape[0] for g in x_groups)
    w_shape = (2, width, wide)
    out = pl.pallas_call(
        lambda *refs: expert_kernel(
            *refs, n_groups=n_groups, n_col=n_col, step_counts=counts, tail=tail),
        name="experts",
        grid=(sum(counts),),
        in_specs=[blocks(k) for k in range(n_groups)] * 2 + [fixed(w_shape)] * n_col + [fixed(select.shape)],
        out_specs=[blocks(k, 2) for k in range(n_groups)] + [fixed(w_shape)] * n_col,
        out_shape=[jax.ShapeDtypeStruct((g.shape[0], 2, rows, model), kind(k)) for k, g in enumerate(x_groups)]
        + [jax.ShapeDtypeStruct(w_shape, F32)] + [jax.ShapeDtypeStruct(w_shape, BF)] * (n_col - 1),
        scratch_shapes=[pltpu.VMEM((2, model, wide), BF), pltpu.VMEM((2, model, wide), F32)],
        cost_estimate=pl.CostEstimate(
            flops=12 * total * rows * model * wide, transcendentals=total * rows * wide,
            bytes_accessed=12 * total * rows * model),
        interpret=interpret,
    )(*x_groups, *go_groups, *weights, select)
    return out[:n_groups], out[n_groups], out[n_groups + 1 :]


def norm_stats(values):
    center = values - jnp.mean(values, axis=1, keepdims=True)
    inverse = lax.rsqrt(jnp.mean(center * center, axis=1, keepdims=True) + epsilon)
    return center * inverse, inverse


def norm_backward(grad_normed, normed, inverse, gain):
    scaled = grad_normed * gain
    grad_values = inverse * (
        scaled
        - jnp.mean(scaled, axis=1, keepdims=True)
        - normed * jnp.mean(scaled * normed, axis=1, keepdims=True)
    )
    return grad_values, jnp.sum(grad_normed * normed, axis=0), jnp.sum(grad_normed, axis=0)


def kept_pairs(choice_ids, order, own_first, own_count, experts, capacity):
    count = order.shape[0]
    numbers = jnp.arange(count, dtype=jnp.int32)
    lanes = jnp.arange(experts, dtype=jnp.int32)[None, :]
    hot_one = (choice_ids[:, 0:1] == lanes).astype(BF)
    hot_two = (choice_ids[:, 1:2] == lanes).astype(BF)
    pick = (order[:, None] == numbers[None, :]).astype(BF)
    ranked = nn(pick, jnp.concatenate([hot_one, hot_two], axis=1)).astype(BF)
    before = (numbers[:, None] > numbers[None, :]).astype(BF)
    earlier = nn(before, ranked)
    totals = jnp.sum(ranked[:, :experts].astype(F32), axis=0, keepdims=True)
    keep_one = ranked[:, :experts] * (earlier[:, :experts] < capacity).astype(BF)
    keep_two = ranked[:, experts:] * (earlier[:, experts:] + totals < capacity).astype(BF)
    own = own_first + jnp.arange(own_count, dtype=jnp.int32)
    pick_own = (own[:, None] == order[None, :]).astype(BF)
    return nn(pick_own, keep_one + keep_two)


def split_two(value):
    high = value.astype(BF)
    return high, (value - high.astype(F32)).astype(BF)


def body(
    tokens, cotangent, expert_ids, priority, qkv_weight, out_weight, attn_gain, attn_shift,
    moe_gain, moe_shift, router, up_weight, down_weight,
):
    rows_sh, width_c = tokens.shape
    n_dp = lax.axis_size("dp")
    n_col = lax.axis_size("col")
    n_row = lax.axis_size("row")
    c = lax.axis_index("col")
    experts = n_dp * E_DEV
    capacity = n_col * max(1, (5 * TOPK * rows_sh + 4 * experts * n_col - 1) // (4 * experts * n_col))
    own = rows_sh // n_col
    images = own // SEQ
    heads_r = qkv_weight.shape[2]
    heads = n_row * heads_r // HDIM
    ff = up_weight.shape[2]
    padded = round_up(own + 2 * experts, 16)
    gate_row = padded - 2 * experts
    score_scale = HDIM ** (-0.5)

    def to_rows(values):
        blocks = values.reshape(n_col, own, width_c)
        got = exchange([lax.dynamic_index_in_dim(blocks, c ^ s, 0, False) for s in range(n_col)], "col")
        return jnp.concatenate(got, axis=1)

    def to_slices(values):
        got = exchange([values[:, s * width_c : (s + 1) * width_c] for s in range(n_col)], "col")
        got = jnp.stack(got)
        return jnp.concatenate(
            [lax.dynamic_index_in_dim(got, c ^ s, 0, False) for s in range(n_col)], axis=0
        )

    stream = to_rows(tokens).astype(F32)

    small = jnp.concatenate(
        [jnp.stack([attn_gain, attn_shift, moe_gain, moe_shift]), router.T,
         jnp.zeros((round_up(4 + experts, 16) - 4 - experts, width_c), BF)], axis=0)
    block = jnp.concatenate(
        [qkv_weight[:, 0], qkv_weight[:, 1], qkv_weight[:, 2], out_weight, small], axis=0)
    by_col = jnp.stack(share(block, "col"))
    small_all = jnp.concatenate([by_col[s, 4 * width_c :] for s in range(n_col)], axis=1).astype(F32)
    g_one, b_one, g_two, b_two = (small_all[i : i + 1] for i in range(4))
    w_router = small_all[4 : 4 + experts].astype(BF)

    grad_out = to_rows(cotangent)
    grad_groups = plane_gather(jnp.pad(grad_out, ((0, padded - own), (0, 0))))
    grad_out = grad_out.astype(F32)

    mine = jnp.stack([up_weight.transpose(1, 0, 2).reshape(width_c, -1),
                      down_weight.transpose(2, 0, 1).reshape(width_c, -1)])
    mine, by_col = lax.optimization_barrier((mine, by_col))
    moe_weights = share(mine, "col")

    by_col = by_col[:, : 4 * width_c]
    by_row = [by_col] + [swap(by_col, "row", s) for s in range(2, n_row, 2)]
    by_row = jnp.stack(by_row)
    near_row = swap(by_row, "row", 1)
    by_row = jnp.stack([by_row, near_row], axis=1).reshape(n_row, n_col, 4, width_c, heads_r)
    w_qkv = by_row[:, :, :3].transpose(1, 3, 2, 0, 4).reshape(D, 3 * n_row * heads_r)
    w_out = by_row[:, :, 3].transpose(0, 2, 1, 3).reshape(n_row * heads_r, D)

    keep = kept_pairs(expert_ids, priority[0], c * own, own, experts, capacity)
    ids_own = lax.dynamic_slice_in_dim(expert_ids, c * own, own, 0)
    lanes = jnp.arange(experts, dtype=jnp.int32)[None, :]
    chosen = (ids_own[:, 0:1] == lanes) | (ids_own[:, 1:2] == lanes)

    normed_one, inverse_one = norm_stats(stream)
    first = (normed_one * g_one + b_one).astype(BF)
    qkv = nn(first, w_qkv).astype(BF).reshape(images, SEQ, 3, heads, HDIM)
    q, k, v = qkv[:, :, 0], qkv[:, :, 1], qkv[:, :, 2]
    scores = jnp.einsum("bqhd,bkhd->bhqk", q, k, preferred_element_type=F32) * score_scale
    raised = jnp.exp(scores - jnp.max(scores, axis=-1, keepdims=True))
    probs = raised / jnp.sum(raised, axis=-1, keepdims=True)
    probs_low = probs.astype(BF)
    attended = (
        jnp.einsum("bhqk,bkhd->bqhd", probs_low, v, preferred_element_type=F32).astype(BF).reshape(own, -1)
    )
    branch = nn(attended, w_out)
    middle = stream + branch
    normed_two, inverse_two = norm_stats(middle)
    second = (normed_two * g_two + b_two).astype(BF)
    logits = nt(second, w_router)
    top = jnp.max(jnp.where(chosen, logits, -jnp.inf), axis=1, keepdims=True)
    lifted = jnp.where(chosen, jnp.exp(jnp.where(chosen, logits - top, 0.0)), 0.0)
    gates = lifted / jnp.sum(lifted, axis=1, keepdims=True)
    gates_kept = gates * keep

    high, low = split_two(gates_kept.T)
    gate_block = jnp.pad(jnp.concatenate([high, low], axis=0), ((0, 0), (0, D - own)))
    block = jnp.concatenate(
        [second, jnp.zeros((gate_row - own, D), BF), gate_block], axis=0)
    x_groups = plane_gather(block)
    tail_start = gate_row // 16 * 16
    tail = padded - tail_start
    row_ids = jnp.arange(tail, dtype=jnp.int32)[:, None] - (gate_row - tail_start)
    expert_of = (
        lax.axis_index("dp") * E_DEV + jnp.arange(E_DEV * ff, dtype=jnp.int32)[None, :] // ff)
    select = jnp.stack([row_ids == expert_of, row_ids - experts == expert_of]).astype(BF)
    moe_sums, moe_own, moe_send = run_experts(x_groups, grad_groups, moe_weights, select)

    def pack_x(value):
        total = value[..., gate_row : gate_row + experts, :] + value[..., gate_row + experts :, :]
        high, low = split_two(total)
        return jnp.concatenate([value[..., :gate_row, :].astype(BF), high, low], axis=-2)

    got, mixture = plane_reduce(moe_sums, pack_x)
    gate_grad = (got[gate_row : gate_row + experts, :own] + got[gate_row + experts :, :own]).T * keep

    moe_got = [swap(moe_send[s - 1], "col", s) for s in range(1, n_col)]

    chosen_grad = gates * (gate_grad - jnp.sum(gates * gate_grad, axis=1, keepdims=True))
    logit_grad = chosen_grad.astype(BF)
    router_grad = tn(logit_grad, second)
    grad_second = got[:own] + nn(logit_grad, w_router)
    grad_norm, g_two_grad, b_two_grad = norm_backward(grad_second, normed_two, inverse_two, g_two)
    grad_middle = grad_out + grad_norm

    grad_branch = grad_middle.astype(BF)
    out_grad = tn(attended, grad_branch)
    grad_attended = nt(grad_branch, w_out).astype(BF).reshape(images, SEQ, heads, HDIM)
    grad_probs = jnp.einsum("bqhd,bkhd->bhqk", grad_attended, v, preferred_element_type=F32)
    grad_v = jnp.einsum("bhqk,bqhd->bkhd", probs_low, grad_attended, preferred_element_type=F32)
    grad_scores = (
        probs * (grad_probs - jnp.sum(probs * grad_probs, axis=-1, keepdims=True))
    ).astype(BF)
    grad_q = jnp.einsum("bhqk,bkhd->bqhd", grad_scores, k, preferred_element_type=F32) * score_scale
    grad_k = jnp.einsum("bhqk,bqhd->bkhd", grad_scores, q, preferred_element_type=F32) * score_scale
    grad_qkv = jnp.stack([grad_q, grad_k, grad_v], axis=2).astype(BF).reshape(own, -1)
    qkv_grad = tn(first, grad_qkv)
    grad_first = nt(grad_qkv, w_qkv)
    grad_norm, g_one_grad, b_one_grad = norm_backward(grad_first, normed_one, inverse_one, g_one)
    tokens_grad = to_slices((grad_middle + grad_norm).astype(BF))
    *mixture, _ = lax.optimization_barrier((*mixture, grad_first))
    mixture = add_up(mixture)[:own]
    output = middle + mixture
    block_out = to_slices(output.astype(BF))

    lane = jnp.arange(D, dtype=jnp.int32) % width_c
    squares = jnp.zeros((D,), F32)
    for i, value in enumerate((stream, branch, middle, mixture, output)):
        squares = squares + jnp.where(lane == i, jnp.sum(value * value), 0.0)
    n_small = round_up(5 + experts, 16)
    small = jnp.concatenate(
        [jnp.stack([g_one_grad, b_one_grad, g_two_grad, b_two_grad]), router_grad, squares[None],
         jnp.zeros((n_small - 5 - experts, D), F32)], axis=0)
    small = jnp.stack([small[:, t * width_c : (t + 1) * width_c] for t in range(n_col)])
    big = jnp.concatenate(
        [qkv_grad.reshape(n_col, width_c, 3, n_row, heads_r).transpose(3, 0, 2, 1, 4),
         out_grad.reshape(n_row, heads_r, n_col, width_c).transpose(0, 2, 1, 3)[:, :, None]], axis=2)
    big = big.reshape(n_row, n_col, 4 * width_c, heads_r)

    def send(big_part, small_part, axis, offset):
        high, low = split_two(small_part)
        message = jnp.concatenate(
            [big_part.astype(BF).reshape(-1, heads_r), high.reshape(-1, heads_r), low.reshape(-1, heads_r)],
            axis=0)
        got = swap(message, axis, offset).astype(F32)
        n_big = big_part.size // heads_r
        n_part = small_part.size // heads_r
        return (got[:n_big].reshape(big_part.shape),
                (got[n_big : n_big + n_part] + got[n_big + n_part :]).reshape(small_part.shape))

    bit = 1
    while bit < n_row:
        halves = big.reshape(big.shape[0] // 2, 2, *big.shape[1:])
        got_big, got_small = send(halves[:, 1], small, "row", bit)
        big, small = halves[:, 0] + got_big, small + got_small
        bit *= 2
    *moe_got, big = lax.optimization_barrier((*moe_got, big))
    moe_total = add_up([moe_own, *moe_got])
    up_grad = moe_total[0].reshape(width_c, E_DEV, ff).transpose(1, 0, 2)
    down_grad = moe_total[1].reshape(width_c, E_DEV, ff).transpose(1, 2, 0)
    big = big[0]
    total_big, total_small = big[0], small[0]
    for s in range(1, n_col):
        got_big, got_small = send(big[s], small[s], "col", s)
        total_big, total_small = total_big + got_big, total_small + got_small
    bit = 1
    while bit < n_dp:
        got_big, got_small = send(total_big, total_small, "dp", bit)
        total_big, total_small = total_big + got_big, total_small + got_small
        bit *= 2
    total_big = total_big.reshape(4, width_c, heads_r)
    qkv_grad = total_big[:3].transpose(1, 0, 2)
    out_grad = total_big[3]
    entries = own * D * n_dp * n_row * n_col
    stream_rms = jnp.sqrt(total_small[4 + experts, :5] / entries)
    return (
        block_out, tokens_grad, qkv_grad, out_grad, total_small[0], total_small[1], total_small[2],
        total_small[3], total_small[4 : 4 + experts].T, up_grad, down_grad, stream_rms,
    )


def solution(mesh):
    in_specs = (
        P(("dp", "row"), "col"), P(("dp", "row"), "col"), P(("dp", "row"), None), P(("dp", "row"), None),
        P("col", None, "row"), P("row", "col"), P("col"), P("col"), P("col"), P("col"), P("col", None),
        P("dp", "col", "row"), P("dp", "row", "col"),
    )
    out_specs = (
        P(("dp", "row"), "col"), P(("dp", "row"), "col"), P("col", None, "row"), P("row", "col"),
        P("col"), P("col"), P("col"), P("col"), P("col", None), P("dp", "col", "row"),
        P("dp", "row", "col"), P(),
    )

    return jax.shard_map(body, mesh=mesh, in_specs=in_specs, out_specs=out_specs, check_vma=False)
```

time: 1530 us -> 292 us (0.19)
  waiting for transfers between devices: 947 us -> 128 us
  blocking collectives: 339 us -> 0 us
  local copies, waits for them, and re-layouts: 95.3 us -> 27.6 us
  starting transfers between devices: 14.3 us -> 70.1 us
  matrix products: 66.2 us -> 17.2 us
  Pallas kernels: 0 us -> 22.8 us
  other arithmetic: 38.6 us -> 22.8 us
    reduce_scatter x4 -> x0, waiting for transfers between devices: 615 us -> none  [the longest x2 539 us: reduce_cols(): lax.psum_scatter(term_fn(jnp.int32(0), local_rows * lax.axis_size('col'))...]
    all_gather x5 -> x0, waiting for transfers between devices: 330 us -> none  [the longest x3 319 us: gather_cols(): return lax.all_gather(values, 'col', axis=0, tiled=True)]
    unnamed x4 -> x0, blocking collectives: 162 us -> none
    ppermute x0 -> x44, waiting for transfers between devices: none -> 128 us  [swap(): return lax.ppermute(value, axis, [(i, i ^ offset) for i in range(size)])]
    psum x8 -> x0, blocking collectives: 125 us -> none  [the longest x6 71.7 us: width_totals(): return lax.psum(values, 'col')]
    ppermute x0 -> x44, starting transfers between devices: none -> 70.1 us  [swap(): return lax.ppermute(value, axis, [(i, i ^ offset) for i in range(size)])]
    dot_general x29 -> x17, matrix products: 66.2 us -> 15.3 us  [the longest x6 4.58 us: nn(): return jnp.dot(a, b, preferred_element_type=F32)]
    gather x10 -> x0, local copies, waits for them, and re-layouts: 42.7 us -> none  [the longest x5 20.6 us: gate_from(): chosen = jnp.take_along_axis(logits, choice_ids, axis=1)]
  transfers between devices with their start and end apart: 16 -> 44, of which waited for: 9 -> 17; matrix products, arithmetic and copies ran while one was open for 8% -> 20% of each run, Pallas kernels for 0% -> 0%
where the time goes in v1:
time: 292 us; the launch traced here: 291 us
  waiting for transfers between devices  128 us (44%)
  starting transfers between devices  70.1 us (24%)
  local copies, waits for them, and re-layouts  27.6 us (9%)
  other arithmetic  22.8 us (8%)
  Pallas kernels  22.8 us (8%)
  matrix products  17.2 us (6%)
    ppermute x44, waiting for transfers between devices, swap(): return lax.ppermute(value, axis, [(i, i ^ offset) for i in range(size)])  128 us
    ppermute x44, starting transfers between devices, swap(): return lax.ppermute(value, axis, [(i, i ^ offset) for i in range(size)])  70.1 us
    pallas_call x1, Pallas kernels, run_experts(): pl.pallas_call(lambda *refs: expert_kernel(*refs, n_groups=n_groups, n_co...  22.8 us
  transfers between devices with their start and end apart: 44, of which 17 were waited for; matrix products, arithmetic and copies ran while one was open for 20% of the time, Pallas kernels for 0%

profile of v1, /device:TPU:0, one launch (start us, length us, event | category | flops | bytes accessed | tf_op | source)
XLA Modules:
  0.0 291.0 jit_solution(10950967818662377689)
XLA Ops:
  1.5 1.6 concatenate.66
  3.1 5.1 %collective-permute-start.5 = (bf16[528,128]{1,0:T(8,128)(2,1)S(1)}, bf16[528,128]{1,0:T(8,128)(2,1)S(1)}, u32[]{:S(2)}, u32[]{:S(2)}) collective-permute-start(bf16[528,128]{1,0:T(8,128)(2,1)S(1)} %concatenate.66), channel_id=1, source_target_pairs={{0,3},{1,2},{2,1},{3,0},{4,7},{5,6},{6,5},{7,4},{8,11},{9,10},{10,... | collective-permute-start | bytes 405512 | tf_op jit(solution)/shard_map/ppermute | solution.py:26
  9.3 2.0 collective-permute-start.14
  12.4 1.4 collective-permute-start.12
  19.0 5.1 %collective-permute-start.3 = (bf16[528,128]{1,0:T(8,128)(2,1)S(1)}, bf16[528,128]{1,0:T(8,128)(2,1)S(1)}, u32[]{:S(2)}, u32[]{:S(2)}) collective-permute-start(bf16[528,128]{1,0:T(8,128)(2,1)S(1)} %concatenate.66), channel_id=1, source_target_pairs={{0,1},{1,0},{2,3},{3,2},{4,5},{5,4},{6,7},{7,6},{8,9},{9,8},{10,11... | collective-permute-start | bytes 405512 | tf_op jit(solution)/shard_map/ppermute | solution.py:26
  24.1 2.5 collective-permute-start.2
  26.7 3.7 %collective-permute-done.2 = bf16[197,128]{1,0:T(8,128)(2,1)S(1)} collective-permute-done((bf16[197,128]{1,0:T(8,128)(2,1)S(1)}, bf16[197,128]{1,0:T(8,128)(2,1)S(1)}, u32[]{:S(2)}, u32[]{:S(2)}) %collective-permute-start.2) | collective-permute-done | bytes 50464 | tf_op jit(solution)/shard_map/ppermute | solution.py:26
  31.7 1.6 collective-permute-start.16
  34.5 1.5 collective-permute-start.15
  36.2 1.5 collective-permute-start.17
  37.9 1.6 collective-permute-start.6
  39.7 14.1 %collective-permute-done.6 = bf16[4,512,128]{2,1,0:T(8,128)(2,1)S(1)} collective-permute-done((bf16[4,512,128]{2,1,0:T(8,128)(2,1)S(1)}, bf16[4,512,128]{2,1,0:T(8,128)(2,1)S(1)}, u32[]{:S(2)}, u32[]{:S(2)}) %collective-permute-start.6) | collective-permute-done | bytes 524320 | tf_op jit(solution)/shard_map/ppermute | solution.py:26
  59.9 1.5 copy.68
  61.4 1.4 convolution_convert_fusion
  64.2 2.0 exponential_reduce_fusion
  69.1 1.5 collective-permute-start.9
  70.6 1.5 collective-permute-start.8
  72.8 4.5 %collective-permute-done.9 = bf16[208,512]{1,0:T(8,128)(2,1)S(1)} collective-permute-done((bf16[208,512]{1,0:T(8,128)(2,1)S(1)}, bf16[208,512]{1,0:T(8,128)(2,1)S(1)}, u32[]{:S(2)}, u32[]{:S(2)}) %collective-permute-start.9) | collective-permute-done | bytes 213024 | tf_op jit(solution)/shard_map/ppermute | solution.py:26
  77.3 4.9 %collective-permute-done.8 = bf16[208,512]{1,0:T(8,128)(2,1)S(1)} collective-permute-done((bf16[208,512]{1,0:T(8,128)(2,1)S(1)}, bf16[208,512]{1,0:T(8,128)(2,1)S(1)}, u32[]{:S(2)}, u32[]{:S(2)}) %collective-permute-start.8) | collective-permute-done | bytes 213024 | tf_op jit(solution)/shard_map/ppermute | solution.py:26
  83.2 3.1 %collective-permute-start.21 = (bf16[2,128,1024]{2,1,0:T(8,128)(2,1)S(1)}, bf16[2,128,1024]{2,1,0:T(8,128)(2,1)S(1)}, u32[]{:S(2)}, u32[]{:S(2)}) collective-permute-start(bf16[2,128,1024]{2,1,0:T(8,128)(2,1)S(1)} %copy-done.21), channel_id=1, source_target_pairs={{0,3},{1,2},{2,1},{3,0},{4,7},{5,6},{6,5},{7,4},{8,11},{9,10},{10,... | collective-permute-start | bytes 1572872 | tf_op jit(solution)/shard_map/ppermute | solution.py:26
  88.4 11.6 %collective-permute-done.21.refs_7_ = bf16[2,128,1024]{2,1,0:T(8,128)(2,1)S(1)} collective-permute-done((bf16[2,128,1024]{2,1,0:T(8,128)(2,1)S(1)}, bf16[2,128,1024]{2,1,0:T(8,128)(2,1)S(1)}, u32[]{:S(2)}, u32[]{:S(2)}) %collective-permute-start.21) | collective-permute-done | bytes 524320 | tf_op jit(solution)/shard_map/ppermute | solution.py:26
  100.0 31.6 %collective-permute-done.20.refs_6_ = bf16[2,128,1024]{2,1,0:T(8,128)(2,1)S(1)} collective-permute-done((bf16[2,128,1024]{2,1,0:T(8,128)(2,1)S(1)}, bf16[2,128,1024]{2,1,0:T(8,128)(2,1)S(1)}, u32[]{:S(2)}, u32[]{:S(2)}) %collective-permute-start.20) | collective-permute-done | bytes 524320 | tf_op jit(solution)/shard_map/ppermute | solution.py:26
  132.6 22.8 %experts.1 = (f32[4,2,208,512]{3,2,1,0:T(8,128)}, bf16[4,2,208,512]{3,2,1,0:T(8,128)(2,1)}, f32[2,128,1024]{2,1,0:T(8,128)}, bf16[2,128,1024]{2,1,0:T(8,128)(2,1...) custom-call(bf16[4,208,512]{2,1,0:T(8,128)(2,1)} %pad_maximum_fusion.4.refs_0_, ...), custom_call_target="tpu_custom_call" | custom-call | flops 10468982784 | bytes 10223616 | tf_op jit(solution)/shard_map/experts/pallas_call | solution.py:189
  156.4 3.0 %collective-permute-done.22 = bf16[4,2,208,512]{3,2,1,0:T(8,128)(2,1)} collective-permute-done((bf16[4,2,208,512]{3,2,1,0:T(8,128)(2,1)}, bf16[4,2,208,512]{3,2,1,0:T(8,128)(2,1)}, u32[]{:S(2)}, u32[]{:S(2)}) %collective-permute-start.22) | collective-permute-done | bytes 1703968 | tf_op jit(solution)/shard_map/ppermute | solution.py:26
  159.4 3.2 %fusion.122 = (bf16[4,1,208,512]{3,2,1,0:T(8,128)(2,1)S(1)}, f32[4,1,208,512]{3,2,1,0:T(8,128)S(1)}, f32[4,1,208,512]{3,2,1,0:T(8,128)S(1)}) fusion(bf16[4,2,208,512]{3,2,1,0:T(8,128)(2,1)} %collective-permute-done.22, f32[4,2,208,512]{3,2,1,0:T(8,128)} %get-tuple-element.30), kind=kLoop, calls=%fused_computation.296 | loop fusion | flops 2129920 | bytes 9371648 | tf_op jit(solution)/shard_map/convert.7
  163.5 1.5 collective-permute-start.25
  166.4 1.7 collective-permute-start.28
  169.5 11.6 %collective-permute-done.26 = bf16[208,512]{1,0:T(8,128)(2,1)S(1)} collective-permute-done((bf16[208,512]{1,0:T(8,128)(2,1)S(1)}, bf16[208,512]{1,0:T(8,128)(2,1)S(1)}, u32[]{:S(2)}, u32[]{:S(2)}) %collective-permute-start.26) | collective-permute-done | bytes 213024 | tf_op jit(solution)/shard_map/ppermute | solution.py:26
  185.6 1.6 convert_bitcast_fusion
  188.2 1.8 copy.69
  190.0 2.5 convolution_bitcast_fusion.2
  192.5 2.2 multiply_reduce_fusion
  196.2 1.5 fusion.128
  197.9 1.7 dot_general.99
  201.2 1.9 multiply_reduce_fusion.4
  204.2 3.2 %fusion.95 = f32[1,512]{1,0:T(1,128)S(1)} fusion(f32[]{:T(128)} %get-tuple-element.51, f32[]{:T(128)} %get-tuple-element.52, f32[]{:T(128)} %get-tuple-element.50, f32[]{:T(128)} %get-tuple-element.102, f32[]{:T(128)} %get-tuple-element.55), kind=kLoop, calls=%fused_computation.264 | loop fusion | flops 10240 | bytes 2068 | tf_op jit(solution)/shard_map/add | solution.py:386
  210.1 2.7 collective-permute-start.31
  212.8 1.8 collective-permute-start.29
  214.9 2.7 collective-permute-start.34
  218.4 1.7 collective-permute-start.32
  221.4 1.5 collective-permute-start.36
  223.4 2.0 collective-permute-start.37
  227.0 6.5 %collective-permute-done.39 = bf16[2176,128]{1,0:T(8,128)(2,1)S(1)} collective-permute-done((bf16[2176,128]{1,0:T(8,128)(2,1)S(1)}, bf16[2176,128]{1,0:T(8,128)(2,1)S(1)}, u32[]{:S(2)}, u32[]{:S(2)}) %collective-permute-start.39) | collective-permute-done | bytes 557088 | tf_op jit(solution)/shard_map/ppermute | solution.py:26
  233.8 24.6 %collective-permute-done.36 = bf16[2,128,1024]{2,1,0:T(8,128)(2,1)S(1)} collective-permute-done((bf16[2,128,1024]{2,1,0:T(8,128)(2,1)S(1)}, bf16[2,128,1024]{2,1,0:T(8,128)(2,1)S(1)}, u32[]{:S(2)}, u32[]{:S(2)}) %collective-permute-start.36) | collective-permute-done | bytes 524320 | tf_op jit(solution)/shard_map/ppermute | solution.py:26
  258.6 2.7 collective-permute-start.42
  261.4 12.7 %collective-permute-start.41 = (bf16[544,128]{1,0:T(8,128)(2,1)S(1)}, bf16[544,128]{1,0:T(8,128)(2,1)S(1)}, u32[]{:S(2)}, u32[]{:S(2)}) collective-permute-start(bf16[544,128]{1,0:T(8,128)(2,1)S(1)} %pad_maximum_fusion.18), channel_id=1, source_target_pairs={{0,2},{1,3},{2,0},{3,1},{4,6},{5,7},{6,4},{7,5},{8,10},{9,11},{10,... | collective-permute-start | bytes 417800 | tf_op jit(solution)/shard_map/ppermute | solution.py:26
  275.7 7.0 %collective-permute-done.41 = bf16[544,128]{1,0:T(8,128)(2,1)S(1)} collective-permute-done((bf16[544,128]{1,0:T(8,128)(2,1)S(1)}, bf16[544,128]{1,0:T(8,128)(2,1)S(1)}, u32[]{:S(2)}, u32[]{:S(2)}) %collective-permute-start.41) | collective-permute-done | bytes 139296 | tf_op jit(solution)/shard_map/ppermute | solution.py:26
  282.8 1.7 collective-permute-start.43
  (337 shorter events, 55.8 us)
Async XLA Ops:
  3.1 33.1 %collective-permute-start.5 = (bf16[528,128]{1,0:T(8,128)(2,1)S(1)}, bf16[528,128]{1,0:T(8,128)(2,1)S(1)}, u32[]{:S(2)}, u32[]{:S(2)}) collective-permute-start(bf16[528,128]{1,0:T(8,128)(2,1)S(1)} %concatenate.66), channel_id=1, source_target_pairs={{0,3},{1,2},{2,1},{3,0},{4,7},{5,6},{6,5},{7,4},{8,11},{9,10},{10,... | collective-permute-start | bytes 405512 | tf_op jit(solution)/shard_map/ppermute | solution.py:26
  8.2 29.4 %collective-permute-start.4 = (bf16[528,128]{1,0:T(8,128)(2,1)S(1)}, bf16[528,128]{1,0:T(8,128)(2,1)S(1)}, u32[]{:S(2)}, u32[]{:S(2)}) collective-permute-start(bf16[528,128]{1,0:T(8,128)(2,1)S(1)} %concatenate.66), channel_id=1, source_target_pairs={{0,2},{1,3},{2,0},{3,1},{4,6},{5,7},{6,4},{7,5},{8,10},{9,11},{10,... | collective-permute-start | bytes 405512 | tf_op jit(solution)/shard_map/ppermute | solution.py:26
  9.3 9.7 %collective-permute-start.14 = (bf16[197,128]{1,0:T(8,128)(2,1)S(1)}, bf16[197,128]{1,0:T(8,128)(2,1)S(1)}, u32[]{:S(2)}, u32[]{:S(2)}) collective-permute-start(bf16[197,128]{1,0:T(8,128)(2,1)S(1)} %get-tuple-element.123), channel_id=1, source_target_pairs={{0,3},{1,2},{2,1},{3,0},{4,7},{5,6},{6,5},{7,4},{8,11},{9,10},{10,... | collective-permute-start | bytes 151304 | tf_op jit(solution)/shard_map/ppermute | solution.py:26
  11.3 12.9 %collective-permute-start.13 = (bf16[197,128]{1,0:T(8,128)(2,1)S(1)}, bf16[197,128]{1,0:T(8,128)(2,1)S(1)}, u32[]{:S(2)}, u32[]{:S(2)}) collective-permute-start(bf16[197,128]{1,0:T(8,128)(2,1)S(1)} %get-tuple-element.124), channel_id=1, source_target_pairs={{0,2},{1,3},{2,0},{3,1},{4,6},{5,7},{6,4},{7,5},{8,10},{9,11},{10,... | collective-permute-start | bytes 151304 | tf_op jit(solution)/shard_map/ppermute | solution.py:26
  12.4 14.3 %collective-permute-start.12 = (bf16[197,128]{1,0:T(8,128)(2,1)S(1)}, bf16[197,128]{1,0:T(8,128)(2,1)S(1)}, u32[]{:S(2)}, u32[]{:S(2)}) collective-permute-start(bf16[197,128]{1,0:T(8,128)(2,1)S(1)} %get-tuple-element.125), channel_id=1, source_target_pairs={{0,1},{1,0},{2,3},{3,2},{4,5},{5,4},{6,7},{7,6},{8,9},{9,8},{10,11... | collective-permute-start | bytes 151304 | tf_op jit(solution)/shard_map/ppermute | solution.py:26
  19.0 18.7 %collective-permute-start.3 = (bf16[528,128]{1,0:T(8,128)(2,1)S(1)}, bf16[528,128]{1,0:T(8,128)(2,1)S(1)}, u32[]{:S(2)}, u32[]{:S(2)}) collective-permute-start(bf16[528,128]{1,0:T(8,128)(2,1)S(1)} %concatenate.66), channel_id=1, source_target_pairs={{0,1},{1,0},{2,3},{3,2},{4,5},{5,4},{6,7},{7,6},{8,9},{9,8},{10,11... | collective-permute-start | bytes 405512 | tf_op jit(solution)/shard_map/ppermute | solution.py:26
  24.1 6.3 %collective-permute-start.2 = (bf16[197,128]{1,0:T(8,128)(2,1)S(1)}, bf16[197,128]{1,0:T(8,128)(2,1)S(1)}, u32[]{:S(2)}, u32[]{:S(2)}) collective-permute-start(bf16[197,128]{1,0:T(8,128)(2,1)S(1)} %get-tuple-element.127), channel_id=1, source_target_pairs={{0,3},{1,2},{2,1},{3,0},{4,7},{5,6},{6,5},{7,4},{8,11},{9,10},{10,... | collective-permute-start | bytes 151304 | tf_op jit(solution)/shard_map/ppermute | solution.py:26
  26.6 5.0 %collective-permute-start.1 = (bf16[197,128]{1,0:T(8,128)(2,1)S(1)}, bf16[197,128]{1,0:T(8,128)(2,1)S(1)}, u32[]{:S(2)}, u32[]{:S(2)}) collective-permute-start(bf16[197,128]{1,0:T(8,128)(2,1)S(1)} %get-tuple-element.128), channel_id=1, source_target_pairs={{0,2},{1,3},{2,0},{3,1},{4,6},{5,7},{6,4},{7,5},{8,10},{9,11},{10,... | collective-permute-start | bytes 151304 | tf_op jit(solution)/shard_map/ppermute | solution.py:26
  30.4 4.1 %collective-permute-start = (bf16[197,128]{1,0:T(8,128)(2,1)S(1)}, bf16[197,128]{1,0:T(8,128)(2,1)S(1)}, u32[]{:S(2)}, u32[]{:S(2)}) collective-permute-start(bf16[197,128]{1,0:T(8,128)(2,1)S(1)} %get-tuple-element.129), channel_id=1, source_target_pairs={{0,1},{1,0},{2,3},{3,2},{4,5},{5,4},{6,7},{7,6},{8,9},{9,8},{10,11... | collective-permute-start | bytes 151304 | tf_op jit(solution)/shard_map/ppermute | solution.py:26
  31.7 22.4 %collective-permute-start.16 = (bf16[208,512]{1,0:T(8,128)(2,1)S(1)}, bf16[208,512]{1,0:T(8,128)(2,1)S(1)}, u32[]{:S(2)}, u32[]{:S(2)}) collective-permute-start(bf16[208,512]{1,0:T(8,128)(2,1)S(1)} %get-tuple-element.121), channel_id=1, source_target_pairs={{0,16},{4,20},{8,24},{12,28},{16,0},{20,4},{24,8},{28,12},{1,17},{... | collective-permute-start | bytes 638984 | tf_op jit(solution)/shard_map/ppermute | solution.py:26
  34.5 19.6 %collective-permute-start.15 = (bf16[208,512]{1,0:T(8,128)(2,1)S(1)}, bf16[208,512]{1,0:T(8,128)(2,1)S(1)}, u32[]{:S(2)}, u32[]{:S(2)}) collective-permute-start(bf16[208,512]{1,0:T(8,128)(2,1)S(1)} %get-tuple-element.121), channel_id=1, source_target_pairs={{0,8},{4,12},{8,0},{12,4},{16,24},{20,28},{24,16},{28,20},{1,9},{5... | collective-permute-start | bytes 638984 | tf_op jit(solution)/shard_map/ppermute | solution.py:26
  36.2 18.0 %collective-permute-start.17 = (bf16[208,512]{1,0:T(8,128)(2,1)S(1)}, bf16[208,512]{1,0:T(8,128)(2,1)S(1)}, u32[]{:S(2)}, u32[]{:S(2)}) collective-permute-start(bf16[208,512]{1,0:T(8,128)(2,1)S(1)} %get-tuple-element.121), channel_id=1, source_target_pairs={{0,24},{4,28},{8,16},{12,20},{16,8},{20,12},{24,0},{28,4},{1,25},{... | collective-permute-start | bytes 638984 | tf_op jit(solution)/shard_map/ppermute | solution.py:26
  37.9 15.9 %collective-permute-start.6 = (bf16[4,512,128]{2,1,0:T(8,128)(2,1)S(1)}, bf16[4,512,128]{2,1,0:T(8,128)(2,1)S(1)}, u32[]{:S(2)}, u32[]{:S(2)}) collective-permute-start(bf16[4,512,128]{2,1,0:T(8,128)(2,1)S(1)} %get-tuple-element.98), channel_id=1, source_target_pairs={{0,8},{4,12},{8,0},{12,4},{1,9},{5,13},{9,1},{13,5},{2,10},{6,14},... | collective-permute-start | bytes 1572872 | tf_op jit(solution)/shard_map/ppermute | solution.py:26
  53.9 2.7 collective-permute-start.7
  54.1 129.2 %copy-start.41 = (f32[1,512]{1,0:T(1,128)}, f32[1,512]{1,0:T(1,128)S(1)}, u32[]{:S(2)}) copy-start(f32[1,512]{1,0:T(1,128)S(1)} %get-tuple-element.141) | copy-start | bytes 6148
  55.1 76.5 %collective-permute-start.18 = (bf16[4,208,512]{2,1,0:T(8,128)(2,1)}, bf16[4,208,512]{2,1,0:T(8,128)(2,1)}, u32[]{:S(2)}, u32[]{:S(2)}) collective-permute-start(bf16[4,208,512]{2,1,0:T(8,128)(2,1)} %pad_maximum_fusion.5.refs_2_), channel_id=1, source_target_pairs={{0,4},{4,0},{8,12},{12,8},{16,20},{20,16},{24,28},{28,24},{1,5},{5... | collective-permute-start | bytes 2555912 | tf_op jit(solution)/shard_map/ppermute | solution.py:26
  68.0 115.3 %copy-start.45 = (f32[197]{0:T(256)}, f32[197]{0:T(256)S(1)}, u32[]{:S(2)}) copy-start(f32[197]{0:T(256)S(1)} %broadcast_multiply_fusion.4) | copy-start | bytes 2368
  68.2 115.1 %copy-start.55 = (f32[197]{0:T(256)}, f32[197]{0:T(256)S(1)}, u32[]{:S(2)}) copy-start(f32[197]{0:T(256)S(1)} %add_rsqrt_fusion) | copy-start | bytes 2368
  68.6 114.8 %copy-start.37 = (f32[197,4]{0,1:T(4,128)}, f32[197,4]{0,1:T(4,128)S(1)}, u32[]{:S(2)}) copy-start(f32[197,4]{0,1:T(4,128)S(1)} %get-tuple-element.157) | copy-start | bytes 9460
  69.1 8.2 %collective-permute-start.9 = (bf16[208,512]{1,0:T(8,128)(2,1)S(1)}, bf16[208,512]{1,0:T(8,128)(2,1)S(1)}, u32[]{:S(2)}, u32[]{:S(2)}) collective-permute-start(bf16[208,512]{1,0:T(8,128)(2,1)S(1)} %pad_maximum_fusion.10), channel_id=1, source_target_pairs={{0,16},{4,20},{8,24},{12,28},{16,0},{20,4},{24,8},{28,12},{1,17},{... | collective-permute-start | bytes 638984 | tf_op jit(solution)/shard_map/ppermute | solution.py:26
  70.6 11.6 %collective-permute-start.8 = (bf16[208,512]{1,0:T(8,128)(2,1)S(1)}, bf16[208,512]{1,0:T(8,128)(2,1)S(1)}, u32[]{:S(2)}, u32[]{:S(2)}) collective-permute-start(bf16[208,512]{1,0:T(8,128)(2,1)S(1)} %pad_maximum_fusion.10), channel_id=1, source_target_pairs={{0,8},{4,12},{8,0},{12,4},{16,24},{20,28},{24,16},{28,20},{1,9},{5... | collective-permute-start | bytes 638984 | tf_op jit(solution)/shard_map/ppermute | solution.py:26
  72.1 10.1 %collective-permute-start.10 = (bf16[208,512]{1,0:T(8,128)(2,1)S(1)}, bf16[208,512]{1,0:T(8,128)(2,1)S(1)}, u32[]{:S(2)}, u32[]{:S(2)}) collective-permute-start(bf16[208,512]{1,0:T(8,128)(2,1)S(1)} %pad_maximum_fusion.10), channel_id=1, source_target_pairs={{0,24},{4,28},{8,16},{12,20},{16,8},{20,12},{24,0},{28,4},{1,25},{... | collective-permute-start | bytes 638984 | tf_op jit(solution)/shard_map/ppermute | solution.py:26
  83.2 49.4 %collective-permute-start.11 = (bf16[4,208,512]{2,1,0:T(8,128)(2,1)}, bf16[4,208,512]{2,1,0:T(8,128)(2,1)}, u32[]{:S(2)}, u32[]{:S(2)}) collective-permute-start(bf16[4,208,512]{2,1,0:T(8,128)(2,1)} %pad_maximum_fusion.4.refs_0_), channel_id=1, source_target_pairs={{0,4},{4,0},{8,12},{12,8},{16,20},{20,16},{24,28},{28,24},{1,5},{5... | collective-permute-start | bytes 2555912 | tf_op jit(solution)/shard_map/ppermute | solution.py:26
  83.2 16.8 %collective-permute-start.21 = (bf16[2,128,1024]{2,1,0:T(8,128)(2,1)S(1)}, bf16[2,128,1024]{2,1,0:T(8,128)(2,1)S(1)}, u32[]{:S(2)}, u32[]{:S(2)}) collective-permute-start(bf16[2,128,1024]{2,1,0:T(8,128)(2,1)S(1)} %copy-done.21), channel_id=1, source_target_pairs={{0,3},{1,2},{2,1},{3,0},{4,7},{5,6},{6,5},{7,4},{8,11},{9,10},{10,... | collective-permute-start | bytes 1572872 | tf_op jit(solution)/shard_map/ppermute | solution.py:26
  86.4 45.2 %collective-permute-start.20 = (bf16[2,128,1024]{2,1,0:T(8,128)(2,1)S(1)}, bf16[2,128,1024]{2,1,0:T(8,128)(2,1)S(1)}, u32[]{:S(2)}, u32[]{:S(2)}) collective-permute-start(bf16[2,128,1024]{2,1,0:T(8,128)(2,1)S(1)} %copy-done.21), channel_id=1, source_target_pairs={{0,2},{1,3},{2,0},{3,1},{4,6},{5,7},{6,4},{7,5},{8,10},{9,11},{10,... | collective-permute-start | bytes 1572872 | tf_op jit(solution)/shard_map/ppermute | solution.py:26
  86.4 45.2 %collective-permute-start.19 = (bf16[2,128,1024]{2,1,0:T(8,128)(2,1)S(1)}, bf16[2,128,1024]{2,1,0:T(8,128)(2,1)S(1)}, u32[]{:S(2)}, u32[]{:S(2)}) collective-permute-start(bf16[2,128,1024]{2,1,0:T(8,128)(2,1)S(1)} %copy-done.21), channel_id=1, source_target_pairs={{0,1},{1,0},{2,3},{3,2},{4,5},{5,4},{6,7},{7,6},{8,9},{9,8},{10,11... | collective-permute-start | bytes 1572872 | tf_op jit(solution)/shard_map/ppermute | solution.py:26
  155.4 4.0 %collective-permute-start.22 = (bf16[4,2,208,512]{3,2,1,0:T(8,128)(2,1)}, bf16[4,2,208,512]{3,2,1,0:T(8,128)(2,1)}, u32[]{:S(2)}, u32[]{:S(2)}) collective-permute-start(bf16[4,2,208,512]{3,2,1,0:T(8,128)(2,1)} %get-tuple-element.31), channel_id=1, source_target_pairs={{0,4},{4,0},{8,12},{12,8},{16,20},{20,16},{24,28},{28,24},{1,5},{5... | collective-permute-start | bytes 5111816 | tf_op jit(solution)/shard_map/ppermute | solution.py:26
  156.4 77.3 %collective-permute-start.35 = (bf16[2,128,1024]{2,1,0:T(8,128)(2,1)}, bf16[2,128,1024]{2,1,0:T(8,128)(2,1)}, u32[]{:S(2)}, u32[]{:S(2)}) collective-permute-start(bf16[2,128,1024]{2,1,0:T(8,128)(2,1)} %get-tuple-element.36), channel_id=1, source_target_pairs={{0,1},{1,0},{2,3},{3,2},{4,5},{5,4},{6,7},{7,6},{8,9},{9,8},{10,11... | collective-permute-start | bytes 1572872 | tf_op jit(solution)/shard_map/ppermute | solution.py:26
  163.5 37.7 %collective-permute-start.25 = (bf16[208,512]{1,0:T(8,128)(2,1)}, bf16[208,512]{1,0:T(8,128)(2,1)}, u32[]{:S(2)}, u32[]{:S(2)}) collective-permute-start(bf16[208,512]{1,0:T(8,128)(2,1)} %get-tuple-element.91), channel_id=1, source_target_pairs={{0,24},{4,28},{8,16},{12,20},{16,8},{20,12},{24,0},{28,4},{1,25},{... | collective-permute-start | bytes 638984 | tf_op jit(solution)/shard_map/ppermute | solution.py:26
  165.2 15.9 %collective-permute-start.26 = (bf16[208,512]{1,0:T(8,128)(2,1)S(1)}, bf16[208,512]{1,0:T(8,128)(2,1)S(1)}, u32[]{:S(2)}, u32[]{:S(2)}) collective-permute-start(bf16[208,512]{1,0:T(8,128)(2,1)S(1)} %get-tuple-element.94), channel_id=1, source_target_pairs={{0,8},{4,12},{8,0},{12,4},{16,24},{20,28},{24,16},{28,20},{1,9},{5... | collective-permute-start | bytes 638984 | tf_op jit(solution)/shard_map/ppermute | solution.py:26
  166.4 15.9 %collective-permute-start.28 = (bf16[208,512]{1,0:T(8,128)(2,1)S(1)}, bf16[208,512]{1,0:T(8,128)(2,1)S(1)}, u32[]{:S(2)}, u32[]{:S(2)}) collective-permute-start(bf16[208,512]{1,0:T(8,128)(2,1)S(1)} %get-tuple-element.95), channel_id=1, source_target_pairs={{0,24},{4,28},{8,16},{12,20},{16,8},{20,12},{24,0},{28,4},{1,25},{... | collective-permute-start | bytes 638984 | tf_op jit(solution)/shard_map/ppermute | solution.py:26
  168.1 15.0 %collective-permute-start.27 = (bf16[208,512]{1,0:T(8,128)(2,1)S(1)}, bf16[208,512]{1,0:T(8,128)(2,1)S(1)}, u32[]{:S(2)}, u32[]{:S(2)}) collective-permute-start(bf16[208,512]{1,0:T(8,128)(2,1)S(1)} %get-tuple-element.96), channel_id=1, source_target_pairs={{0,16},{4,20},{8,24},{12,28},{16,0},{20,4},{24,8},{28,12},{1,17},{... | collective-permute-start | bytes 638984 | tf_op jit(solution)/shard_map/ppermute | solution.py:26
  181.1 20.1 %collective-permute-start.24 = (bf16[208,512]{1,0:T(8,128)(2,1)}, bf16[208,512]{1,0:T(8,128)(2,1)}, u32[]{:S(2)}, u32[]{:S(2)}) collective-permute-start(bf16[208,512]{1,0:T(8,128)(2,1)} %get-tuple-element.92), channel_id=1, source_target_pairs={{0,16},{4,20},{8,24},{12,28},{16,0},{20,4},{24,8},{28,12},{1,17},{... | collective-permute-start | bytes 638984 | tf_op jit(solution)/shard_map/ppermute | solution.py:26
  182.3 18.9 %collective-permute-start.23 = (bf16[208,512]{1,0:T(8,128)(2,1)}, bf16[208,512]{1,0:T(8,128)(2,1)}, u32[]{:S(2)}, u32[]{:S(2)}) collective-permute-start(bf16[208,512]{1,0:T(8,128)(2,1)} %get-tuple-element.93), channel_id=1, source_target_pairs={{0,8},{4,12},{8,0},{12,4},{16,24},{20,28},{24,16},{28,20},{1,9},{5... | collective-permute-start | bytes 638984 | tf_op jit(solution)/shard_map/ppermute | solution.py:26
  210.0 4.9 %collective-permute-start.38 = (bf16[4224,128]{1,0:T(8,128)(2,1)S(1)}, bf16[4224,128]{1,0:T(8,128)(2,1)S(1)}, u32[]{:S(2)}, u32[]{:S(2)}) collective-permute-start(bf16[4224,128]{1,0:T(8,128)(2,1)S(1)} %pad_maximum_fusion.2), channel_id=1, source_target_pairs={{0,4},{4,0},{8,12},{12,8},{1,5},{5,1},{9,13},{13,9},{2,6},{6,2},{1... | collective-permute-start | bytes 3244040 | tf_op jit(solution)/shard_map/ppermute | solution.py:26
  210.1 8.2 %collective-permute-start.31 = (bf16[197,128]{1,0:T(8,128)(2,1)S(1)}, bf16[197,128]{1,0:T(8,128)(2,1)S(1)}, u32[]{:S(2)}, u32[]{:S(2)}) collective-permute-start(bf16[197,128]{1,0:T(8,128)(2,1)S(1)} %get-tuple-element.117), channel_id=1, source_target_pairs={{0,3},{1,2},{2,1},{3,0},{4,7},{5,6},{6,5},{7,4},{8,11},{9,10},{10,... | collective-permute-start | bytes 151304 | tf_op jit(solution)/shard_map/ppermute | solution.py:26
  212.8 5.6 %collective-permute-start.30 = (bf16[197,128]{1,0:T(8,128)(2,1)S(1)}, bf16[197,128]{1,0:T(8,128)(2,1)S(1)}, u32[]{:S(2)}, u32[]{:S(2)}) collective-permute-start(bf16[197,128]{1,0:T(8,128)(2,1)S(1)} %get-tuple-element.118), channel_id=1, source_target_pairs={{0,2},{1,3},{2,0},{3,1},{4,6},{5,7},{6,4},{7,5},{8,10},{9,11},{10,... | collective-permute-start | bytes 151304 | tf_op jit(solution)/shard_map/ppermute | solution.py:26
  212.8 7.4 %collective-permute-start.29 = (bf16[197,128]{1,0:T(8,128)(2,1)S(1)}, bf16[197,128]{1,0:T(8,128)(2,1)S(1)}, u32[]{:S(2)}, u32[]{:S(2)}) collective-permute-start(bf16[197,128]{1,0:T(8,128)(2,1)S(1)} %get-tuple-element.119), channel_id=1, source_target_pairs={{0,1},{1,0},{2,3},{3,2},{4,5},{5,4},{6,7},{7,6},{8,9},{9,8},{10,11... | collective-permute-start | bytes 151304 | tf_op jit(solution)/shard_map/ppermute | solution.py:26
  214.9 6.5 %collective-permute-start.34 = (bf16[197,128]{1,0:T(8,128)(2,1)S(1)}, bf16[197,128]{1,0:T(8,128)(2,1)S(1)}, u32[]{:S(2)}, u32[]{:S(2)}) collective-permute-start(bf16[197,128]{1,0:T(8,128)(2,1)S(1)} %get-tuple-element.109), channel_id=1, source_target_pairs={{0,3},{1,2},{2,1},{3,0},{4,7},{5,6},{6,5},{7,4},{8,11},{9,10},{10,... | collective-permute-start | bytes 151304 | tf_op jit(solution)/shard_map/ppermute | solution.py:26
  218.3 5.1 %collective-permute-start.33 = (bf16[197,128]{1,0:T(8,128)(2,1)S(1)}, bf16[197,128]{1,0:T(8,128)(2,1)S(1)}, u32[]{:S(2)}, u32[]{:S(2)}) collective-permute-start(bf16[197,128]{1,0:T(8,128)(2,1)S(1)} %get-tuple-element.110), channel_id=1, source_target_pairs={{0,2},{1,3},{2,0},{3,1},{4,6},{5,7},{6,4},{7,5},{8,10},{9,11},{10,... | collective-permute-start | bytes 151304 | tf_op jit(solution)/shard_map/ppermute | solution.py:26
  218.4 7.0 %collective-permute-start.32 = (bf16[197,128]{1,0:T(8,128)(2,1)S(1)}, bf16[197,128]{1,0:T(8,128)(2,1)S(1)}, u32[]{:S(2)}, u32[]{:S(2)}) collective-permute-start(bf16[197,128]{1,0:T(8,128)(2,1)S(1)} %get-tuple-element.111), channel_id=1, source_target_pairs={{0,1},{1,0},{2,3},{3,2},{4,5},{5,4},{6,7},{7,6},{8,9},{9,8},{10,11... | collective-permute-start | bytes 151304 | tf_op jit(solution)/shard_map/ppermute | solution.py:26
  220.1 13.3 %collective-permute-start.39 = (bf16[2176,128]{1,0:T(8,128)(2,1)S(1)}, bf16[2176,128]{1,0:T(8,128)(2,1)S(1)}, u32[]{:S(2)}, u32[]{:S(2)}) collective-permute-start(bf16[2176,128]{1,0:T(8,128)(2,1)S(1)} %pad_maximum_fusion.7), channel_id=1, source_target_pairs={{0,8},{4,12},{8,0},{12,4},{1,9},{5,13},{9,1},{13,5},{2,10},{6,14},... | collective-permute-start | bytes 1671176 | tf_op jit(solution)/shard_map/ppermute | solution.py:26
  221.4 37.0 %collective-permute-start.36 = (bf16[2,128,1024]{2,1,0:T(8,128)(2,1)S(1)}, bf16[2,128,1024]{2,1,0:T(8,128)(2,1)S(1)}, u32[]{:S(2)}, u32[]{:S(2)}) collective-permute-start(bf16[2,128,1024]{2,1,0:T(8,128)(2,1)S(1)} %copy-done.66), channel_id=1, source_target_pairs={{0,2},{1,3},{2,0},{3,1},{4,6},{5,7},{6,4},{7,5},{8,10},{9,11},{10,... | collective-permute-start | bytes 1572872 | tf_op jit(solution)/shard_map/ppermute | solution.py:26
  223.4 34.9 %collective-permute-start.37 = (bf16[2,128,1024]{2,1,0:T(8,128)(2,1)S(1)}, bf16[2,128,1024]{2,1,0:T(8,128)(2,1)S(1)}, u32[]{:S(2)}, u32[]{:S(2)}) collective-permute-start(bf16[2,128,1024]{2,1,0:T(8,128)(2,1)S(1)} %copy-done.65), channel_id=1, source_target_pairs={{0,3},{1,2},{2,1},{3,0},{4,7},{5,6},{6,5},{7,4},{8,11},{9,10},{10,... | collective-permute-start | bytes 1572872 | tf_op jit(solution)/shard_map/ppermute | solution.py:26
  258.6 17.0 %collective-permute-start.42 = (bf16[544,128]{1,0:T(8,128)(2,1)S(1)}, bf16[544,128]{1,0:T(8,128)(2,1)S(1)}, u32[]{:S(2)}, u32[]{:S(2)}) collective-permute-start(bf16[544,128]{1,0:T(8,128)(2,1)S(1)} %pad_maximum_fusion.19), channel_id=1, source_target_pairs={{0,3},{1,2},{2,1},{3,0},{4,7},{5,6},{6,5},{7,4},{8,11},{9,10},{10,... | collective-permute-start | bytes 417800 | tf_op jit(solution)/shard_map/ppermute | solution.py:26
  261.4 21.3 %collective-permute-start.41 = (bf16[544,128]{1,0:T(8,128)(2,1)S(1)}, bf16[544,128]{1,0:T(8,128)(2,1)S(1)}, u32[]{:S(2)}, u32[]{:S(2)}) collective-permute-start(bf16[544,128]{1,0:T(8,128)(2,1)S(1)} %pad_maximum_fusion.18), channel_id=1, source_target_pairs={{0,2},{1,3},{2,0},{3,1},{4,6},{5,7},{6,4},{7,5},{8,10},{9,11},{10,... | collective-permute-start | bytes 417800 | tf_op jit(solution)/shard_map/ppermute | solution.py:26
  274.1 8.6 %collective-permute-start.40 = (bf16[544,128]{1,0:T(8,128)(2,1)S(1)}, bf16[544,128]{1,0:T(8,128)(2,1)S(1)}, u32[]{:S(2)}, u32[]{:S(2)}) collective-permute-start(bf16[544,128]{1,0:T(8,128)(2,1)S(1)} %pad_maximum_fusion.17), channel_id=1, source_target_pairs={{0,1},{1,0},{2,3},{3,2},{4,5},{5,4},{6,7},{7,6},{8,9},{9,8},{10,11... | collective-permute-start | bytes 417800 | tf_op jit(solution)/shard_map/ppermute | solution.py:26
  282.8 5.1 %collective-permute-start.43 = (bf16[544,128]{1,0:T(8,128)(2,1)S(1)}, bf16[544,128]{1,0:T(8,128)(2,1)S(1)}, u32[]{:S(2)}, u32[]{:S(2)}) collective-permute-start(bf16[544,128]{1,0:T(8,128)(2,1)S(1)} %pad_maximum_fusion.20), channel_id=1, source_target_pairs={{0,16},{16,0},{1,17},{17,1},{2,18},{18,2},{3,19},{19,3},{4,20},{20... | collective-permute-start | bytes 417800 | tf_op jit(solution)/shard_map/ppermute | solution.py:26
  (66 other events, 1069.0 us)
